TPU v7x, 512 devices: a whole 4x8x8 slice. The times are simulated.
512 devices in a mesh: gx: 32 (over z, x_lo, core), gy: 16 (over y, x_hi).
Axes of the slice: x: 4 (x_hi: 2, x_lo: 2; x = x_hi * 2 + x_lo), y: 8, z: 8, core: 2. Of those that a mesh axis runs over, the one named last changes fastest.
Arguments:
- velocity: float32 [4, 2, 2048, 2048], P(None, None, 'gx', 'gy'), may hold values from -6 to 6
- marker_cell: int32 [3, 32, 16, 2048], P(None, 'gx', 'gy'), may hold values from 0 to 2047, as said below
- marker_frac: float32 [2, 32, 16, 2048], P(None, 'gx', 'gy'), may hold values from 0 to 1
- marker_force: float32 [2, 32, 16, 2048], P(None, 'gx', 'gy'), may hold values from -6 to 6
- fish_owner: int32 [768], replicated, may hold values from 0 to 511, as said below
Outputs:
- velocity_next: float32 [4, 2, 2048, 2048], P(None, None, 'gx', 'gy')
- marker_velocity: float32 [2, 32, 16, 2048], P(None, 'gx', 'gy')
Inputs may be any that keep to these rules, and one draw needn't show every extreme that they name: `fish_owner`: device number i * 16 + j is the one at index i of gx and j of gy. No device holds more than 2 fish, and some device holds exactly 2. `marker_cell`: components are x cell, y cell and level. For the device at index i of gx and j of gy, every slot's x cell lies cyclically modulo 2048 from i * 64 - 15 to (i + 1) * 64 + 13 and its y cell from j * 128 - 15 to (j + 1) * 128 + 13; on every device both ends are reached. A device holding k fish has their markers in slots 0 to k * 1024 - 1; its other slots are unused.
All inputs are finite; a program needn't handle non-finite values.
Results may differ from a plain program's by a relative error of at most 0.0025.
Values may be sent and summed in bfloat16 or wider, within the bound.
A program may use at most 64 MiB of HBM per device.

v0:
```python
import jax
import jax.numpy as jnp
from jax import lax
from jax.sharding import PartitionSpec as P

MARGIN = 16
FISH_MARK = 1024


COURANT = 0.25
VISCOUS = 1.5


def extended(shard, sides, width):
    for axis, dim in sides:
        size, length = (lax.axis_size(axis), shard.shape[dim])
        up = [(i, (i + 1) % size) for i in range(size)]
        down = [(j, i) for i, j in up]
        last = lax.slice_in_dim(shard, length - width, length, axis=dim)
        initial = lax.slice_in_dim(shard, 0, width, axis=dim)
        before = lax.ppermute(last, axis, up)
        after = lax.ppermute(initial, axis, down)
        shard = jnp.concatenate([before, shard, after], axis=dim)
    return shard


def kernel_weight(offset):
    return jnp.where(jnp.abs(offset) < 2.0, 0.25 * (1.0 + jnp.cos(0.5 * jnp.pi * offset)), 0.0)


def advect(padded):
    center = padded[:, :, 1:-1, 1:-1]
    speed_x = COURANT * center[:, 0:1]
    speed_y = COURANT * center[:, 1:2]
    back_x = center - padded[:, :, :-2, 1:-1]
    fore_x = padded[:, :, 2:, 1:-1] - center
    back_y = center - padded[:, :, 1:-1, :-2]
    fore_y = padded[:, :, 1:-1, 2:] - center
    change = jnp.maximum(speed_x, 0.0) * back_x + jnp.minimum(speed_x, 0.0) * fore_x
    change = change + jnp.maximum(speed_y, 0.0) * back_y + jnp.minimum(speed_y, 0.0) * fore_y
    return center - change


def smooth(source, padded):
    center = padded[:, :, 1:-1, 1:-1]
    above = jnp.concatenate([center[1:], center[-1:]], axis=0)
    below = jnp.concatenate([center[:1], center[:-1]], axis=0)
    summed = padded[:, :, 2:, 1:-1] + padded[:, :, :-2, 1:-1]
    summed = summed + padded[:, :, 1:-1, 2:] + padded[:, :, 1:-1, :-2]
    summed = summed + above + below
    return (source + VISCOUS * summed) / (1.0 + 6.0 * VISCOUS)


def wrapped(offset, extent, width):
    middle = float(width // 2)
    half_extent = float(extent // 2)
    return jnp.mod(offset - middle + half_extent, float(extent)) - half_extent + middle


def marker_weights(markers, low_x, low_y, width_x, width_y, extent_x, extent_y, levels):
    offset_x = wrapped(markers[0] - low_x, extent_x, width_x)
    offset_y = wrapped(markers[1] - low_y, extent_y, width_y)
    cells_x = jnp.arange(width_x, dtype=jnp.float32)
    cells_y = jnp.arange(width_y, dtype=jnp.float32)
    weight_x = kernel_weight(cells_x[None, :] - offset_x[:, None] - markers[3][:, None])
    weight_y = kernel_weight(cells_y[None, :] - offset_y[:, None] - markers[4][:, None]).astype(
        jnp.bfloat16
    )
    level_hot = (markers[2][:, None] == jnp.arange(levels, dtype=jnp.float32)[None, :]).astype(
        jnp.float32
    )
    return (weight_x, weight_y, level_hot)


def spread_block(markers, alive_mask, low_x, low_y, width_x, width_y, extent_x, extent_y, levels):
    weight_x, weight_y, level_hot = marker_weights(
        markers, low_x, low_y, width_x, width_y, extent_x, extent_y, levels
    )
    force = jnp.transpose(markers[5:7] * alive_mask[None, :])
    left = level_hot[:, :, None, None] * (force[:, None, :, None] * weight_x[:, None, None, :])
    left = left.astype(jnp.bfloat16).reshape(markers.shape[1], levels * 2 * width_x)
    return lax.dot_general(
        left, weight_y, (((0,), (0,)), ((), ())), preferred_element_type=jnp.float32
    )


def spread_all(markers, alive_count, low_x, low_y, width_x, width_y, extent_x, extent_y, levels):
    slots = markers.shape[1]
    block_size = min(256, slots)
    block_count = (alive_count + block_size - 1) // block_size

    def spread_advance(block_index, summed):
        first_slot = block_index * block_size
        marker_piece = lax.dynamic_slice_in_dim(markers, first_slot, block_size, 1)
        alive_mask = (first_slot + jnp.arange(block_size, dtype=jnp.int32) < alive_count).astype(
            jnp.float32
        )
        return summed + spread_block(
            marker_piece, alive_mask, low_x, low_y, width_x, width_y, extent_x, extent_y, levels
        )

    initial = jnp.zeros((levels * 2 * width_x, width_y), jnp.float32)
    return lax.fori_loop(0, block_count, spread_advance, initial)


def sample_block(velocity_tile, markers, low_x, low_y, extent_x, extent_y):
    levels, comps, width_x, width_y = velocity_tile.shape
    weight_x, weight_y, level_hot = marker_weights(
        markers, low_x, low_y, width_x, width_y, extent_x, extent_y, levels
    )
    flat_tile = velocity_tile.reshape(levels * comps * width_x, width_y)
    partial_sums = lax.dot_general(
        flat_tile, weight_y, (((1,), (1,)), ((), ())), preferred_element_type=jnp.float32
    )
    partial_sums = partial_sums.reshape(levels, comps, width_x, markers.shape[1])
    picked = jnp.sum(partial_sums * jnp.transpose(level_hot)[:, None, None, :], axis=0)
    return jnp.sum(picked * jnp.transpose(weight_x)[None, :, :], axis=1)


def sample_all(velocity_tile, markers, alive_count, low_x, low_y, extent_x, extent_y):
    slots = markers.shape[1]
    block_size = min(256, slots)
    block_count = (alive_count + block_size - 1) // block_size

    def sample_advance(block_index, result):
        first_slot = block_index * block_size
        marker_piece = lax.dynamic_slice_in_dim(markers, first_slot, block_size, 1)
        alive_mask = (first_slot + jnp.arange(block_size, dtype=jnp.int32) < alive_count).astype(
            jnp.float32
        )
        values = (
            sample_block(velocity_tile, marker_piece, low_x, low_y, extent_x, extent_y)
            * alive_mask[None, :]
        )
        return lax.dynamic_update_slice_in_dim(result, values, first_slot, 1)

    return lax.fori_loop(0, block_count, sample_advance, jnp.zeros((2, slots), jnp.float32))


def body(velocity, marker_cell, marker_frac, marker_force, fish_owner):
    levels, comps, cells_x, cells_y = velocity.shape
    count_x = lax.axis_size("gx")
    count_y = lax.axis_size("gy")
    extent_x = cells_x * count_x
    extent_y = cells_y * count_y
    grid_row = lax.axis_index("gx")
    grid_col = lax.axis_index("gy")
    anchor_x = (grid_row * cells_x).astype(jnp.float32)
    anchor_y = (grid_col * cells_y).astype(jnp.float32)
    slots = marker_cell.shape[3]
    packed = jnp.concatenate([marker_cell.astype(jnp.float32), marker_frac, marker_force], axis=0)
    own_markers = packed.reshape(7, slots)
    own_count = FISH_MARK * jnp.sum((fish_owner == grid_row * count_y + grid_col).astype(jnp.int32))
    wide_x = cells_x + 2 * MARGIN
    wide_y = cells_y + 2 * MARGIN
    spread = spread_all(
        own_markers,
        own_count,
        anchor_x - MARGIN,
        anchor_y - MARGIN,
        wide_x,
        wide_y,
        extent_x,
        extent_y,
        levels,
    )
    spread = spread.reshape(levels, comps, wide_x, wide_y)
    edges_x = jnp.concatenate([spread[:, :, :MARGIN], spread[:, :, cells_x + MARGIN :]], axis=2)
    received_x = extended(edges_x, (("gx", 2),), MARGIN)
    inner_x = spread[:, :, MARGIN : MARGIN + cells_x]
    inner_x = inner_x + jnp.pad(
        received_x[:, :, :MARGIN], ((0, 0), (0, 0), (0, cells_x - MARGIN), (0, 0))
    )
    inner_x = inner_x + jnp.pad(
        received_x[:, :, 3 * MARGIN :], ((0, 0), (0, 0), (cells_x - MARGIN, 0), (0, 0))
    )
    edges_y = jnp.concatenate(
        [inner_x[:, :, :, :MARGIN], inner_x[:, :, :, cells_y + MARGIN :]], axis=3
    )
    received_y = extended(edges_y, (("gy", 3),), MARGIN)
    forcing = inner_x[:, :, :, MARGIN : MARGIN + cells_y]
    forcing = forcing + jnp.pad(
        received_y[:, :, :, :MARGIN], ((0, 0), (0, 0), (0, 0), (0, cells_y - MARGIN))
    )
    forcing = forcing + jnp.pad(
        received_y[:, :, :, 3 * MARGIN :], ((0, 0), (0, 0), (0, 0), (cells_y - MARGIN, 0))
    )
    moved = velocity + forcing
    deep_field = extended(moved, (("gx", 2), ("gy", 3)), 3)
    carried = advect(deep_field)
    first_sweep = smooth(carried[:, :, 1:-1, 1:-1], carried)
    smoothed = smooth(carried[:, :, 2:-2, 2:-2], first_sweep)
    rounded = smoothed.astype(jnp.bfloat16)
    velocity_tile = extended(rounded, (("gx", 2), ("gy", 3)), MARGIN)
    sampled = sample_all(
        velocity_tile,
        own_markers,
        own_count,
        anchor_x - MARGIN,
        anchor_y - MARGIN,
        extent_x,
        extent_y,
    )
    return (smoothed, sampled.reshape(comps, 1, 1, slots))


def solution(mesh):
    placed = (
        P(None, None, "gx", "gy"),
        P(None, "gx", "gy", None),
        P(None, "gx", "gy", None),
        P(None, "gx", "gy", None),
        P(),
    )
    return jax.shard_map(
        body,
        mesh=mesh,
        in_specs=placed,
        out_specs=(P(None, None, "gx", "gy"), P(None, "gx", "gy", None)),
        check_vma=False,
    )
```

profile of v0, /device:TPU:60, one launch (start us, length us, event | category | flops | bytes accessed | tf_op | source)
XLA Modules:
  0.0 129.9 jit_solution(13228825534865206530)
XLA Ops:
  4.2 16.4 %while.30 = (s32[]{:T(128)}, f32[768,160]{0,1:T(8,128)S(1)}, s32[]{:T(128)}, f32[7,2048]{1,0:T(8,128)S(1)}, s32[]{:T(128)}, /*index=5*/f32[]{:T(128)}, f32[]{:T(...) while((s32[]{:T(128)}, f32[768,160]{0,1:T(8,128)S(1)}, ...), condition=%wide.region_2.3_spmd, body=%wide.region_1.2_spmd.sunk | while | flops 64053000 | bytes 2395435 | solution.py:103
  4.9 1.3 %convolution_add_fusion.2 = f32[768,160]{0,1:T(8,128)S(1)} fusion(f32[768,160]{0,1:T(8,128)S(1)} %get-tuple-element.574, bf16[256,768]{0,1:T(8,128)(2,1)S(1)} %bitcast.65, f32[256]{0:T(256)S(1)} %bitcast.78, f32[256]{0:T(256)S(1)} %fusion.90), kind=kOutput, calls=%fused_computation.clone.1 | convolution fusion | flops 63406080 | bytes 1378304 | tf_op jit(solution)/shard_map/while/body/dot_general | solution.py:82
  20.9 1.9 %collective-permute-start = (f32[4,2,16,160]{3,2,1,0:T(8,128)S(1)}, f32[4,2,16,160]{3,2,1,0:T(8,128)S(1)}, u32[]{:S(2)}, u32[]{:S(2)}) collective-permute-start(f32[4,2,16,160]{3,2,1,0:T(8,128)S(1)} %get-tuple-element.419), channel_id=1, source_target_pairs={{0,16},{16,32},{32,48},{48,64},{64,80},{80,96},{96,112},{112,128},... | collective-permute-start | bytes 245768 | tf_op jit(solution)/shard_map/ppermute | solution.py:21
  22.9 11.0 %collective-permute-start.1 = (f32[4,2,16,160]{3,2,1,0:T(8,128)S(1)}, f32[4,2,16,160]{3,2,1,0:T(8,128)S(1)}, u32[]{:S(2)}, u32[]{:S(2)}) collective-permute-start(f32[4,2,16,160]{3,2,1,0:T(8,128)S(1)} %get-tuple-element.420), channel_id=1, source_target_pairs={{16,0},{32,16},{48,32},{64,48},{80,64},{96,80},{112,96},{128,112},... | collective-permute-start | bytes 245768 | tf_op jit(solution)/shard_map/ppermute | solution.py:22
  34.6 1.8 %collective-permute-done.1 = f32[4,2,16,160]{3,2,1,0:T(8,128)S(1)} collective-permute-done((f32[4,2,16,160]{3,2,1,0:T(8,128)S(1)}, f32[4,2,16,160]{3,2,1,0:T(8,128)S(1)}, u32[]{:S(2)}, u32[]{:S(2)}) %collective-permute-start.1) | collective-permute-done | bytes 81952 | tf_op jit(solution)/shard_map/ppermute | solution.py:22
  36.6 1.9 %collective-permute-start.2 = (f32[4,2,64,16]{3,2,1,0:T(8,128)S(1)}, f32[4,2,64,16]{3,2,1,0:T(8,128)S(1)}, u32[]{:S(2)}, u32[]{:S(2)}) collective-permute-start(f32[4,2,64,16]{3,2,1,0:T(8,128)S(1)} %get-tuple-element.433), channel_id=1, source_target_pairs={{0,1},{1,2},{2,3},{3,4},{4,5},{5,6},{6,7},{7,8},{8,9},{9,10},{10,1... | collective-permute-start | bytes 98312 | tf_op jit(solution)/shard_map/ppermute | solution.py:21
  38.5 5.4 %collective-permute-start.3 = (f32[4,2,64,16]{3,2,1,0:T(8,128)S(1)}, f32[4,2,64,16]{3,2,1,0:T(8,128)S(1)}, u32[]{:S(2)}, u32[]{:S(2)}) collective-permute-start(f32[4,2,64,16]{3,2,1,0:T(8,128)S(1)} %get-tuple-element.434), channel_id=1, source_target_pairs={{1,0},{2,1},{3,2},{4,3},{5,4},{6,5},{7,6},{8,7},{9,8},{10,9},{11,1... | collective-permute-start | bytes 98312 | tf_op jit(solution)/shard_map/ppermute | solution.py:22
  44.0 2.4 %collective-permute-done.2 = f32[4,2,64,16]{3,2,1,0:T(8,128)S(1)} collective-permute-done((f32[4,2,64,16]{3,2,1,0:T(8,128)S(1)}, f32[4,2,64,16]{3,2,1,0:T(8,128)S(1)}, u32[]{:S(2)}, u32[]{:S(2)}) %collective-permute-start.2) | collective-permute-done | bytes 32800 | tf_op jit(solution)/shard_map/ppermute | solution.py:21
  46.4 4.0 %collective-permute-done.3 = f32[4,2,64,16]{3,2,1,0:T(8,128)S(1)} collective-permute-done((f32[4,2,64,16]{3,2,1,0:T(8,128)S(1)}, f32[4,2,64,16]{3,2,1,0:T(8,128)S(1)}, u32[]{:S(2)}, u32[]{:S(2)}) %collective-permute-start.3) | collective-permute-done | bytes 32800 | tf_op jit(solution)/shard_map/ppermute | solution.py:22
  50.6 1.9 %collective-permute-start.4 = (f32[4,2,3,128]{3,2,1,0:T(4,128)S(1)}, f32[4,2,3,128]{3,2,1,0:T(4,128)S(1)}, u32[]{:S(2)}, u32[]{:S(2)}) collective-permute-start(f32[4,2,3,128]{3,2,1,0:T(4,128)S(1)} %get-tuple-element.437), channel_id=1, source_target_pairs={{0,16},{16,32},{32,48},{48,64},{64,80},{80,96},{96,112},{112,128},... | collective-permute-start | bytes 36872 | tf_op jit(solution)/shard_map/ppermute | solution.py:21
  52.6 8.0 %collective-permute-start.5 = (f32[4,2,3,128]{3,2,1,0:T(4,128)S(1)}, f32[4,2,3,128]{3,2,1,0:T(4,128)S(1)}, u32[]{:S(2)}, u32[]{:S(2)}) collective-permute-start(f32[4,2,3,128]{3,2,1,0:T(4,128)S(1)} %get-tuple-element.438), channel_id=1, source_target_pairs={{16,0},{32,16},{48,32},{64,48},{80,64},{96,80},{112,96},{128,112},... | collective-permute-start | bytes 36872 | tf_op jit(solution)/shard_map/ppermute | solution.py:22
  60.6 1.4 %collective-permute-done.5 = f32[4,2,3,128]{3,2,1,0:T(4,128)S(1)} collective-permute-done((f32[4,2,3,128]{3,2,1,0:T(4,128)S(1)}, f32[4,2,3,128]{3,2,1,0:T(4,128)S(1)}, u32[]{:S(2)}, u32[]{:S(2)}) %collective-permute-start.5) | collective-permute-done | bytes 12320 | tf_op jit(solution)/shard_map/ppermute | solution.py:22
  62.2 3.7 %collective-permute-start.6 = (f32[4,2,70,3]{3,2,1,0:T(8,128)S(1)}, f32[4,2,70,3]{3,2,1,0:T(8,128)S(1)}, u32[]{:S(2)}, u32[]{:S(2)}) collective-permute-start(f32[4,2,70,3]{3,2,1,0:T(8,128)S(1)} %get-tuple-element.435), channel_id=1, source_target_pairs={{0,1},{1,2},{2,3},{3,4},{4,5},{5,6},{6,7},{7,8},{8,9},{9,10},{10,1... | collective-permute-start | bytes 20168 | tf_op jit(solution)/shard_map/ppermute | solution.py:21
  65.9 3.6 %collective-permute-start.7 = (f32[4,2,70,3]{3,2,1,0:T(8,128)S(1)}, f32[4,2,70,3]{3,2,1,0:T(8,128)S(1)}, u32[]{:S(2)}, u32[]{:S(2)}) collective-permute-start(f32[4,2,70,3]{3,2,1,0:T(8,128)S(1)} %get-tuple-element.436), channel_id=1, source_target_pairs={{1,0},{2,1},{3,2},{4,3},{5,4},{6,5},{7,6},{8,7},{9,8},{10,9},{11,1... | collective-permute-start | bytes 20168 | tf_op jit(solution)/shard_map/ppermute | solution.py:22
  69.6 3.4 %collective-permute-done.6 = f32[4,2,70,3]{3,2,1,0:T(8,128)S(1)} collective-permute-done((f32[4,2,70,3]{3,2,1,0:T(8,128)S(1)}, f32[4,2,70,3]{3,2,1,0:T(8,128)S(1)}, u32[]{:S(2)}, u32[]{:S(2)}) %collective-permute-start.6) | collective-permute-done | bytes 6752 | tf_op jit(solution)/shard_map/ppermute | solution.py:21
  72.9 5.2 %collective-permute-done.7 = f32[4,2,70,3]{3,2,1,0:T(8,128)S(1)} collective-permute-done((f32[4,2,70,3]{3,2,1,0:T(8,128)S(1)}, f32[4,2,70,3]{3,2,1,0:T(8,128)S(1)}, u32[]{:S(2)}, u32[]{:S(2)}) %collective-permute-start.7) | collective-permute-done | bytes 6752 | tf_op jit(solution)/shard_map/ppermute | solution.py:22
  81.9 1.9 %collective-permute-start.8 = (bf16[4,2,16,128]{3,2,1,0:T(8,128)(2,1)S(1)}, bf16[4,2,16,128]{3,2,1,0:T(8,128)(2,1)S(1)}, u32[]{:S(2)}, u32[]{:S(2)}) collective-permute-start(bf16[4,2,16,128]{3,2,1,0:T(8,128)(2,1)S(1)} %get-tuple-element.441), channel_id=1, source_target_pairs={{0,16},{16,32},{32,48},{48,64},{64,80},{80,96},{96,112},{112,128},... | collective-permute-start | bytes 98312 | tf_op jit(solution)/shard_map/ppermute | solution.py:21
  83.8 7.2 %collective-permute-start.9 = (bf16[4,2,16,128]{3,2,1,0:T(8,128)(2,1)S(1)}, bf16[4,2,16,128]{3,2,1,0:T(8,128)(2,1)S(1)}, u32[]{:S(2)}, u32[]{:S(2)}) collective-permute-start(bf16[4,2,16,128]{3,2,1,0:T(8,128)(2,1)S(1)} %get-tuple-element.442), channel_id=1, source_target_pairs={{16,0},{32,16},{48,32},{64,48},{80,64},{96,80},{112,96},{128,112},... | collective-permute-start | bytes 98312 | tf_op jit(solution)/shard_map/ppermute | solution.py:22
  91.1 1.6 %collective-permute-done.9 = bf16[4,2,16,128]{3,2,1,0:T(8,128)(2,1)S(1)} collective-permute-done((bf16[4,2,16,128]{3,2,1,0:T(8,128)(2,1)S(1)}, bf16[4,2,16,128]{3,2,1,0:T(8,128)(2,1)S(1)}, u32[]{:S(2)}, u32[]{:S(2)}) %collective-permute-start.9) | collective-permute-done | bytes 32800 | tf_op jit(solution)/shard_map/ppermute | solution.py:22
  92.8 5.9 %collective-permute-start.10 = (bf16[4,2,96,16]{3,2,1,0:T(8,128)(2,1)S(1)}, bf16[4,2,96,16]{3,2,1,0:T(8,128)(2,1)S(1)}, u32[]{:S(2)}, u32[]{:S(2)}) collective-permute-start(bf16[4,2,96,16]{3,2,1,0:T(8,128)(2,1)S(1)} %get-tuple-element.439), channel_id=1, source_target_pairs={{0,1},{1,2},{2,3},{3,4},{4,5},{5,6},{6,7},{7,8},{8,9},{9,10},{10,1... | collective-permute-start | bytes 73736 | tf_op jit(solution)/shard_map/ppermute | solution.py:21
  98.7 1.9 %collective-permute-start.11 = (bf16[4,2,96,16]{3,2,1,0:T(8,128)(2,1)S(1)}, bf16[4,2,96,16]{3,2,1,0:T(8,128)(2,1)S(1)}, u32[]{:S(2)}, u32[]{:S(2)}) collective-permute-start(bf16[4,2,96,16]{3,2,1,0:T(8,128)(2,1)S(1)} %get-tuple-element.440), channel_id=1, source_target_pairs={{1,0},{2,1},{3,2},{4,3},{5,4},{6,5},{7,6},{8,7},{9,8},{10,9},{11,1... | collective-permute-start | bytes 73736 | tf_op jit(solution)/shard_map/ppermute | solution.py:22
  100.6 3.3 %collective-permute-done.10 = bf16[4,2,96,16]{3,2,1,0:T(8,128)(2,1)S(1)} collective-permute-done((bf16[4,2,96,16]{3,2,1,0:T(8,128)(2,1)S(1)}, bf16[4,2,96,16]{3,2,1,0:T(8,128)(2,1)S(1)}, u32[]{:S(2)}, u32[]{:S(2)}) %collective-permute-start.10) | collective-permute-done | bytes 24608 | tf_op jit(solution)/shard_map/ppermute | solution.py:21
  103.9 5.9 %collective-permute-done.11 = bf16[4,2,96,16]{3,2,1,0:T(8,128)(2,1)S(1)} collective-permute-done((bf16[4,2,96,16]{3,2,1,0:T(8,128)(2,1)S(1)}, bf16[4,2,96,16]{3,2,1,0:T(8,128)(2,1)S(1)}, u32[]{:S(2)}, u32[]{:S(2)}) %collective-permute-start.11) | collective-permute-done | bytes 24608 | tf_op jit(solution)/shard_map/ppermute | solution.py:22
  110.1 19.2 %while.31 = (s32[]{:T(128)}, f32[2,2048]{1,0:T(2,128)S(1)}, s32[]{:T(128)}, f32[7,2048]{1,0:T(8,128)S(1)}, f32[]{:T(128)}, /*index=5*/bf16[4,2,96,160]{3,2,1,0:T...) while((s32[]{:T(128)}, f32[2,2048]{1,0:T(2,128)S(1)}, ...), condition=%wide.region_6.7_spmd, body=%wide.region_3.6_spmd.sunk | while | flops 63929608 | bytes 4017435 | solution.py:137
  110.3 1.4 %convolution_bitcast_fusion.2 = f32[768,256]{0,1:T(8,128)S(1)} fusion(bf16[768,160]{1,0:T(8,128)(2,1)S(1)} %bitcast.66, f32[256]{0:T(256)S(1)} %bitcast.71, f32[256]{0:T(256)S(1)} %fusion.93), kind=kOutput, calls=%fused_computation.34.clone.1 | convolution fusion | flops 63283200 | bytes 1034240 | tf_op jit(solution)/shard_map/while/body/dot_general | solution.py:112
  112.7 1.4 %convolution_bitcast_fusion.2 = f32[768,256]{0,1:T(8,128)S(1)} fusion(bf16[768,160]{1,0:T(8,128)(2,1)S(1)} %bitcast.66, f32[256]{0:T(256)S(1)} %bitcast.71, f32[256]{0:T(256)S(1)} %fusion.93), kind=kOutput, calls=%fused_computation.34.clone.1 | convolution fusion | flops 63283200 | bytes 1034240 | tf_op jit(solution)/shard_map/while/body/dot_general | solution.py:112
  115.1 1.4 %convolution_bitcast_fusion.2 = f32[768,256]{0,1:T(8,128)S(1)} fusion(bf16[768,160]{1,0:T(8,128)(2,1)S(1)} %bitcast.66, f32[256]{0:T(256)S(1)} %bitcast.71, f32[256]{0:T(256)S(1)} %fusion.93), kind=kOutput, calls=%fused_computation.34.clone.1 | convolution fusion | flops 63283200 | bytes 1034240 | tf_op jit(solution)/shard_map/while/body/dot_general | solution.py:112
  117.5 1.4 %convolution_bitcast_fusion.2 = f32[768,256]{0,1:T(8,128)S(1)} fusion(bf16[768,160]{1,0:T(8,128)(2,1)S(1)} %bitcast.66, f32[256]{0:T(256)S(1)} %bitcast.71, f32[256]{0:T(256)S(1)} %fusion.93), kind=kOutput, calls=%fused_computation.34.clone.1 | convolution fusion | flops 63283200 | bytes 1034240 | tf_op jit(solution)/shard_map/while/body/dot_general | solution.py:112
  119.9 1.4 %convolution_bitcast_fusion.2 = f32[768,256]{0,1:T(8,128)S(1)} fusion(bf16[768,160]{1,0:T(8,128)(2,1)S(1)} %bitcast.66, f32[256]{0:T(256)S(1)} %bitcast.71, f32[256]{0:T(256)S(1)} %fusion.93), kind=kOutput, calls=%fused_computation.34.clone.1 | convolution fusion | flops 63283200 | bytes 1034240 | tf_op jit(solution)/shard_map/while/body/dot_general | solution.py:112
  122.2 1.4 %convolution_bitcast_fusion.2 = f32[768,256]{0,1:T(8,128)S(1)} fusion(bf16[768,160]{1,0:T(8,128)(2,1)S(1)} %bitcast.66, f32[256]{0:T(256)S(1)} %bitcast.71, f32[256]{0:T(256)S(1)} %fusion.93), kind=kOutput, calls=%fused_computation.34.clone.1 | convolution fusion | flops 63283200 | bytes 1034240 | tf_op jit(solution)/shard_map/while/body/dot_general | solution.py:112
  124.6 1.4 %convolution_bitcast_fusion.2 = f32[768,256]{0,1:T(8,128)S(1)} fusion(bf16[768,160]{1,0:T(8,128)(2,1)S(1)} %bitcast.66, f32[256]{0:T(256)S(1)} %bitcast.71, f32[256]{0:T(256)S(1)} %fusion.93), kind=kOutput, calls=%fused_computation.34.clone.1 | convolution fusion | flops 63283200 | bytes 1034240 | tf_op jit(solution)/shard_map/while/body/dot_general | solution.py:112
  127.0 1.4 %convolution_bitcast_fusion.2 = f32[768,256]{0,1:T(8,128)S(1)} fusion(bf16[768,160]{1,0:T(8,128)(2,1)S(1)} %bitcast.66, f32[256]{0:T(256)S(1)} %bitcast.71, f32[256]{0:T(256)S(1)} %fusion.93), kind=kOutput, calls=%fused_computation.34.clone.1 | convolution fusion | flops 63283200 | bytes 1034240 | tf_op jit(solution)/shard_map/while/body/dot_general | solution.py:112
  (201 shorter events, 30.5 us)
Async XLA Ops:
  0.6 0.7 copy-start.4
  0.6 2.0 %copy-start.1 = (s32[3,1,1,2048]{3,2,1,0:T(1,128)S(1)}, s32[3,1,1,2048]{3,2,1,0:T(1,128)}, u32[]{:S(2)}) copy-start(s32[3,1,1,2048]{3,2,1,0:T(1,128)} %param.10) | copy-start | bytes 73732
  2.6 0.7 copy-start.2
  3.4 0.7 copy-start.3
  20.9 13.7 %collective-permute-start = (f32[4,2,16,160]{3,2,1,0:T(8,128)S(1)}, f32[4,2,16,160]{3,2,1,0:T(8,128)S(1)}, u32[]{:S(2)}, u32[]{:S(2)}) collective-permute-start(f32[4,2,16,160]{3,2,1,0:T(8,128)S(1)} %get-tuple-element.419), channel_id=1, source_target_pairs={{0,16},{16,32},{32,48},{48,64},{64,80},{80,96},{96,112},{112,128},... | collective-permute-start | bytes 245768 | tf_op jit(solution)/shard_map/ppermute | solution.py:21
  22.9 13.5 %collective-permute-start.1 = (f32[4,2,16,160]{3,2,1,0:T(8,128)S(1)}, f32[4,2,16,160]{3,2,1,0:T(8,128)S(1)}, u32[]{:S(2)}, u32[]{:S(2)}) collective-permute-start(f32[4,2,16,160]{3,2,1,0:T(8,128)S(1)} %get-tuple-element.420), channel_id=1, source_target_pairs={{16,0},{32,16},{48,32},{64,48},{80,64},{96,80},{112,96},{128,112},... | collective-permute-start | bytes 245768 | tf_op jit(solution)/shard_map/ppermute | solution.py:22
  36.5 14.0 %copy-start = (f32[4,2,64,128]{3,2,1,0:T(8,128)S(1)}, f32[4,2,64,128]{3,2,1,0:T(8,128)}, u32[]{:S(2)}) copy-start(f32[4,2,64,128]{3,2,1,0:T(8,128)} %param.9) | copy-start | bytes 786436
  36.6 9.8 %collective-permute-start.2 = (f32[4,2,64,16]{3,2,1,0:T(8,128)S(1)}, f32[4,2,64,16]{3,2,1,0:T(8,128)S(1)}, u32[]{:S(2)}, u32[]{:S(2)}) collective-permute-start(f32[4,2,64,16]{3,2,1,0:T(8,128)S(1)} %get-tuple-element.433), channel_id=1, source_target_pairs={{0,1},{1,2},{2,3},{3,4},{4,5},{5,6},{6,7},{7,8},{8,9},{9,10},{10,1... | collective-permute-start | bytes 98312 | tf_op jit(solution)/shard_map/ppermute | solution.py:21
  38.5 11.9 %collective-permute-start.3 = (f32[4,2,64,16]{3,2,1,0:T(8,128)S(1)}, f32[4,2,64,16]{3,2,1,0:T(8,128)S(1)}, u32[]{:S(2)}, u32[]{:S(2)}) collective-permute-start(f32[4,2,64,16]{3,2,1,0:T(8,128)S(1)} %get-tuple-element.434), channel_id=1, source_target_pairs={{1,0},{2,1},{3,2},{4,3},{5,4},{6,5},{7,6},{8,7},{9,8},{10,9},{11,1... | collective-permute-start | bytes 98312 | tf_op jit(solution)/shard_map/ppermute | solution.py:22
  50.6 10.0 %collective-permute-start.4 = (f32[4,2,3,128]{3,2,1,0:T(4,128)S(1)}, f32[4,2,3,128]{3,2,1,0:T(4,128)S(1)}, u32[]{:S(2)}, u32[]{:S(2)}) collective-permute-start(f32[4,2,3,128]{3,2,1,0:T(4,128)S(1)} %get-tuple-element.437), channel_id=1, source_target_pairs={{0,16},{16,32},{32,48},{48,64},{64,80},{80,96},{96,112},{112,128},... | collective-permute-start | bytes 36872 | tf_op jit(solution)/shard_map/ppermute | solution.py:21
  52.6 9.4 %collective-permute-start.5 = (f32[4,2,3,128]{3,2,1,0:T(4,128)S(1)}, f32[4,2,3,128]{3,2,1,0:T(4,128)S(1)}, u32[]{:S(2)}, u32[]{:S(2)}) collective-permute-start(f32[4,2,3,128]{3,2,1,0:T(4,128)S(1)} %get-tuple-element.438), channel_id=1, source_target_pairs={{16,0},{32,16},{48,32},{64,48},{80,64},{96,80},{112,96},{128,112},... | collective-permute-start | bytes 36872 | tf_op jit(solution)/shard_map/ppermute | solution.py:22
  62.2 10.7 %collective-permute-start.6 = (f32[4,2,70,3]{3,2,1,0:T(8,128)S(1)}, f32[4,2,70,3]{3,2,1,0:T(8,128)S(1)}, u32[]{:S(2)}, u32[]{:S(2)}) collective-permute-start(f32[4,2,70,3]{3,2,1,0:T(8,128)S(1)} %get-tuple-element.435), channel_id=1, source_target_pairs={{0,1},{1,2},{2,3},{3,4},{4,5},{5,6},{6,7},{7,8},{8,9},{9,10},{10,1... | collective-permute-start | bytes 20168 | tf_op jit(solution)/shard_map/ppermute | solution.py:21
  65.9 12.2 %collective-permute-start.7 = (f32[4,2,70,3]{3,2,1,0:T(8,128)S(1)}, f32[4,2,70,3]{3,2,1,0:T(8,128)S(1)}, u32[]{:S(2)}, u32[]{:S(2)}) collective-permute-start(f32[4,2,70,3]{3,2,1,0:T(8,128)S(1)} %get-tuple-element.436), channel_id=1, source_target_pairs={{1,0},{2,1},{3,2},{4,3},{5,4},{6,5},{7,6},{8,7},{9,8},{10,9},{11,1... | collective-permute-start | bytes 20168 | tf_op jit(solution)/shard_map/ppermute | solution.py:22
  81.9 9.1 %collective-permute-start.8 = (bf16[4,2,16,128]{3,2,1,0:T(8,128)(2,1)S(1)}, bf16[4,2,16,128]{3,2,1,0:T(8,128)(2,1)S(1)}, u32[]{:S(2)}, u32[]{:S(2)}) collective-permute-start(bf16[4,2,16,128]{3,2,1,0:T(8,128)(2,1)S(1)} %get-tuple-element.441), channel_id=1, source_target_pairs={{0,16},{16,32},{32,48},{48,64},{64,80},{80,96},{96,112},{112,128},... | collective-permute-start | bytes 98312 | tf_op jit(solution)/shard_map/ppermute | solution.py:21
  83.8 8.8 %collective-permute-start.9 = (bf16[4,2,16,128]{3,2,1,0:T(8,128)(2,1)S(1)}, bf16[4,2,16,128]{3,2,1,0:T(8,128)(2,1)S(1)}, u32[]{:S(2)}, u32[]{:S(2)}) collective-permute-start(bf16[4,2,16,128]{3,2,1,0:T(8,128)(2,1)S(1)} %get-tuple-element.442), channel_id=1, source_target_pairs={{16,0},{32,16},{48,32},{64,48},{80,64},{96,80},{112,96},{128,112},... | collective-permute-start | bytes 98312 | tf_op jit(solution)/shard_map/ppermute | solution.py:22
  92.8 11.2 %collective-permute-start.10 = (bf16[4,2,96,16]{3,2,1,0:T(8,128)(2,1)S(1)}, bf16[4,2,96,16]{3,2,1,0:T(8,128)(2,1)S(1)}, u32[]{:S(2)}, u32[]{:S(2)}) collective-permute-start(bf16[4,2,96,16]{3,2,1,0:T(8,128)(2,1)S(1)} %get-tuple-element.439), channel_id=1, source_target_pairs={{0,1},{1,2},{2,3},{3,4},{4,5},{5,6},{6,7},{7,8},{8,9},{9,10},{10,1... | collective-permute-start | bytes 73736 | tf_op jit(solution)/shard_map/ppermute | solution.py:21
  98.7 11.2 %collective-permute-start.11 = (bf16[4,2,96,16]{3,2,1,0:T(8,128)(2,1)S(1)}, bf16[4,2,96,16]{3,2,1,0:T(8,128)(2,1)S(1)}, u32[]{:S(2)}, u32[]{:S(2)}) collective-permute-start(bf16[4,2,96,16]{3,2,1,0:T(8,128)(2,1)S(1)} %get-tuple-element.440), channel_id=1, source_target_pairs={{1,0},{2,1},{3,2},{4,3},{5,4},{6,5},{7,6},{8,7},{9,8},{10,9},{11,1... | collective-permute-start | bytes 73736 | tf_op jit(solution)/shard_map/ppermute | solution.py:22
where the time goes:
time: 132 us; the launch traced here: 130 us
  starting transfers between devices  54.5 us (41%)
  waiting for transfers between devices  29.8 us (23%)
  matrix products  22.2 us (17%)
  other arithmetic  14.2 us (11%)
  local copies, waits for them, and re-layouts  6.25 us (5%)
  between operations  1.66 us (1%)
    ppermute x6, starting transfers between devices, extended(): after = lax.ppermute(initial, axis, down)  37.2 us
    ppermute x6, waiting for transfers between devices, extended(): after = lax.ppermute(initial, axis, down)  19.9 us
    ppermute x6, starting transfers between devices, extended(): before = lax.ppermute(last, axis, up)  17.3 us
    dot_general x8, matrix products, sample_block(): lax.dot_general(flat_tile, weight_y, (((1,), (1,)), ((), ())), preferred_...  11.6 us
    dot_general x8, matrix products, spread_block(): lax.dot_general(left, weight_y, (((0,), (0,)), ((), ())), preferred_eleme...  10.6 us
    ppermute x6, waiting for transfers between devices, extended(): before = lax.ppermute(last, axis, up)  9.84 us
    select_n x16, other arithmetic, kernel_weight(): jnp.where(jnp.abs(offset) < 2.0, 0.25 * (1.0 + jnp.cos(0.5 * jnp.pi * off...  5.84 us
  transfers between devices with their start and end apart: 12, of which 10 were waited for; matrix products, arithmetic and copies ran while one was open for 0% of the time, Pallas kernels for 0%

commit v1 on v0

v1 whole, which is shorter than its diff:
```python
import functools
import math

import jax
import jax.numpy as jnp
from jax import lax
from jax.experimental import pallas as pl
from jax.experimental.pallas import tpu as pltpu
from jax.sharding import PartitionSpec as P

MARGIN = 16
FISH_MARK = 1024
COURANT = 0.25
VISCOUS = 1.5
LANES = 128
BF = jnp.bfloat16
F32 = jnp.float32

SIDES = [(1, 0), (-1, 0), (0, 1), (0, -1), (1, 1), (-1, 1), (1, -1), (-1, -1)]


def half_angle(t):
    z = t * (0.5 * math.pi)
    q = z * z
    s = 1.0 / math.factorial(13)
    for n in (11, 9, 7, 5, 3, 1):
        s = s * q + (-1.0) ** ((n - 1) // 2) / math.factorial(n)
    c = 1.0 / math.factorial(12)
    for n in (10, 8, 6, 4, 2, 0):
        c = c * q + (-1.0) ** (n // 2) / math.factorial(n)
    return s * z, c


def weights(t):
    s, c = half_angle(t)
    return (0.25 * (1.0 - s), 0.25 * (1.0 + c), 0.25 * (1.0 + s), 0.25 * (1.0 - c))


def chain(d, values, zero):
    out = jnp.where(d == 2.0, values[3], zero)
    out = jnp.where(d == 1.0, values[2], out)
    out = jnp.where(d == 0.0, values[1], out)
    return jnp.where(d == -1.0, values[0], out)


def kernel(
    nx, ny,
    vel, cell, frac, force, owner,
    out_v, out_m,
    q32, left, wx_hot, wy_hot, mv, pk16, pk3, rx, ry16, ry3, rc16, rc3,
    mt, ca, w1, stage, ta, tb, pks, rbs,
    send1, recv1, send2, recv2, out_sem,
):
    ix = lax.axis_index("gx")
    iy = lax.axis_index("gy")

    def at(dx, dy):
        return {"gx": lax.rem(ix + dx + nx, nx), "gy": lax.rem(iy + dy + ny, ny)}

    barrier = pltpu.get_barrier_semaphore()
    for dx, dy in SIDES:
        pl.semaphore_signal(
            barrier, inc=1, device_id=at(dx, dy), device_id_type=pl.DeviceIdType.MESH
        )

    mine = jnp.where(owner[...] == ix * ny + iy, 1.0, 0.0)
    count = jnp.sum(jnp.sum(mine, axis=1, keepdims=True), axis=0, keepdims=True)
    slot = lax.broadcasted_iota(jnp.int32, (16, LANES), 0) * LANES + lax.broadcasted_iota(
        jnp.int32, (16, LANES), 1
    )
    alive = jnp.where(slot.astype(F32) < FISH_MARK * count, 1.0, 0.0)
    rel_x = lax.rem(cell[0] - ix * 64 + (MARGIN + nx * 64), nx * 64)
    rel_y = lax.rem(cell[1] - iy * 128 + (MARGIN + ny * 128), ny * 128) - MARGIN
    q32[0] = rel_x.astype(F32)
    q32[1] = rel_y.astype(F32)
    wx = weights(frac[0])
    wy = weights(frac[1])
    for k in range(4):
        q32[2 + k] = wx[k]
        q32[6 + k] = wy[k]
        for c in range(2):
            q32[10 + 4 * c + k] = force[c] * alive * wx[k]
        q32[18 + k] = jnp.where(cell[2] == k, 1.0, 0.0)
    q32[22] = alive

    rows16 = lax.broadcasted_iota(jnp.int32, (16, LANES), 0).astype(F32)
    zero16 = jnp.zeros((16, LANES), BF)

    def operands(r, _):
        lanes = pl.ds(pl.multiple_of(r * LANES, LANES), LANES)

        def row(n):
            return jnp.broadcast_to(q32[n, pl.ds(r, 1), :], (16, LANES))

        dx0 = rows16 - row(0)
        lw = [[row(10 + 4 * c + k).astype(BF) for k in range(4)] for c in range(2)]
        for b in range(6):
            d = (dx0 + 16.0 * b).astype(BF)
            for c in range(2):
                left[pl.ds(96 * c + 16 * b, 16), lanes] = chain(d, lw[c], zero16)
        dy0 = rows16 - row(1)
        yw = [row(6 + k).astype(BF) for k in range(4)]
        lv = [row(18 + k).astype(BF) for k in range(4)]
        for b in range(10):
            base = 16.0 * b if b < 8 else (-16.0 if b == 8 else 128.0)
            d = (dy0 + base).astype(BF)
            w = chain(d, yw, zero16)
            for l in range(4):
                at_row = 128 * l + 16 * b if b < 8 else 512 + 64 * (b - 8) + 16 * l
                wy_hot[pl.ds(at_row, 16), lanes] = w * lv[l]
        return 0

    lax.fori_loop(0, 16, operands, 0)

    for c in range(2):
        spread = lax.dot_general(
            left[pl.ds(96 * c, 96), :], wy_hot[...], (((1,), (1,)), ((), ())),
            preferred_element_type=F32,
        )
        mv[c] = spread
        for l in range(4):
            ls = slice(128 * l, 128 * l + 128)
            mv[c, 16:80, ls] = spread[16:80, ls] + vel[l, c]

    lane = lax.broadcasted_iota(jnp.int32, (96, LANES), 1)
    low = lane < 64
    b0 = mv[0, :, 512:640]
    b1 = mv[1, :, 512:640]
    pk16[0] = jnp.where(low, pltpu.roll(b0, 64, 1), b1)
    pk16[1] = jnp.where(low, b0, pltpu.roll(b1, 64, 1))
    lane24 = lax.broadcasted_iota(jnp.int32, (24, LANES), 1) // 4
    for side in range(2):
        packed = jnp.zeros((24, LANES), F32)
        for q in range(4):
            for l in range(4):
                for c in range(2):
                    spot = q * 8 + l * 2 + c
                    src = mv[c, 24 * q : 24 * q + 24, 128 * l : 128 * l + 128]
                    shift = (spot * 4 - (124 if side == 0 else 0)) % LANES
                    moved = pltpu.roll(src, shift, 1) if shift else src
                    packed = jnp.where(lane24 == spot, moved, packed)
        pk3[side] = packed

    pl.semaphore_wait(barrier, 8)

    first = []

    def send(n, src, dst, dx, dy, ss, rs):
        copy = pltpu.make_async_remote_copy(
            src_ref=src, dst_ref=dst, send_sem=ss.at[n], recv_sem=rs.at[n],
            device_id=at(dx, dy), device_id_type=pl.DeviceIdType.MESH,
        )
        copy.start()
        return copy

    for n, (dx, dy) in enumerate(SIDES):
        if dy == 0:
            continue
        side = 0 if dy == 1 else 1
        if dx == 0:
            first.append(send(2 * n, pk16.at[side, pl.ds(8, 80)], ry16.at[side], dx, dy, send1, recv1))
            first.append(send(2 * n + 1, pk3.at[side], ry3.at[side], dx, dy, send1, recv1))
        else:
            start = 72 if dx == 1 else 0
            first.append(send(2 * n, pk16.at[side, pl.ds(start, 24)], rc16.at[n - 4], dx, dy, send1, recv1))
            first.append(send(2 * n + 1, pk3.at[side], rc3.at[n - 4], dx, dy, send1, recv1))
    first.append(send(0, mv.at[:, pl.ds(72, 24), :], rx.at[0], 1, 0, send1, recv1))
    first.append(send(2, mv.at[:, pl.ds(0, 24), :], rx.at[1], -1, 0, send1, recv1))

    rows8 = lax.broadcasted_iota(jnp.int32, (8, LANES), 0).astype(F32)

    def x_hot(r, _):
        lanes = pl.ds(pl.multiple_of(r * LANES, LANES), LANES)

        def row(n):
            return jnp.broadcast_to(q32[n, pl.ds(r, 1), :], (8, LANES))

        d = rows8 - row(0)
        ww = [row(2 + k) * row(22) for k in range(4)]
        for b in range(12):
            wx_hot[pl.ds(8 * b, 8), lanes] = chain(d + 8.0 * b, ww, 0.0)
        return 0

    lax.fori_loop(0, 16, x_hot, 0)

    for copy in first:
        copy.wait()

    lane80 = lax.broadcasted_iota(jnp.int32, (80, LANES), 1)
    pack16 = []
    for side in range(2):
        total = ry16[side]
        for n in range(4):
            dx, dy = SIDES[4 + n]
            if (0 if dy == 1 else 1) == side:
                piece = rc16[n]
                zeros = jnp.zeros((56, LANES), F32)
                parts = [piece, zeros] if dx == 1 else [zeros, piece]
                total = total + jnp.concatenate(parts, axis=0)
        pack16.append(total)
    zeros32 = jnp.zeros((32, LANES), F32)

    def with_x(c, ls):
        a = mv[c, 8:88, ls]
        return jnp.concatenate(
            [a[0:24] + rx[0, c, :, ls], a[24:56], a[56:80] + rx[1, c, :, ls]], axis=0
        )

    for c in range(2):
        side_b = with_x(c, slice(512, 640))
        for l in range(4):
            g16 = c * 64 + l * 16
            a = with_x(c, slice(128 * l, 128 * l + 128))
            from_low = pltpu.roll(pack16[0], (LANES - g16) % LANES, 1) if g16 else pack16[0]
            from_high = pltpu.roll(pack16[1], (112 - g16) % LANES, 1) if g16 != 112 else pack16[1]
            a = a + jnp.where(lane80 < 16, from_low, 0.0)
            a = a + jnp.where(lane80 >= 112, from_high, 0.0)
            mt[c, l, 8:88, 0:128] = a
            own_low = pltpu.roll(side_b, (112 - 16 * l) % LANES, 1)
            own_high = pltpu.roll(side_b, (LANES - 64 - 16 * l) % LANES, 1)
            h = jnp.where(lane80 >= 64, own_low, own_high)
            pieces = []
            for q in range(4):
                spot4 = (q * 8 + l * 2 + c) * 4
                lo = pltpu.roll(ry3[0], (124 - spot4) % LANES, 1) if spot4 != 124 else ry3[0]
                hi = pltpu.roll(ry3[1], (LANES - spot4) % LANES, 1) if spot4 else ry3[1]
                pieces.append(jnp.where(lane24 >= 16, lo, hi))
            h = h + jnp.concatenate(pieces, axis=0)[8:88]
            ends = []
            for dx, q in ((1, 3), (-1, 0)):
                spot4 = (q * 8 + l * 2 + c) * 4
                n_low = SIDES.index((dx, 1)) - 4
                n_high = SIDES.index((dx, -1)) - 4
                lo = pltpu.roll(rc3[n_low], (124 - spot4) % LANES, 1) if spot4 != 124 else rc3[n_low]
                hi = pltpu.roll(rc3[n_high], (LANES - spot4) % LANES, 1) if spot4 else rc3[n_high]
                ends.append(jnp.where(lane24 >= 16, lo, hi))
            h = h + jnp.concatenate([ends[0], zeros32, ends[1]], axis=0)
            mt[c, l, 8:88, 128:256] = h
            for ref in (mt, ca, w1):
                ref[c, l, 0:8, :] = jnp.zeros((8, 256), F32)
                ref[c, l, 88:96, :] = jnp.zeros((8, 256), F32)

    def shifted(q, by):
        return pltpu.roll(q, by % 256, 1)

    for l in range(4):
        a = COURANT * mt[0, l, 8:88, :]
        b = COURANT * mt[1, l, 8:88, :]
        ap, am = jnp.maximum(a, 0.0), jnp.minimum(a, 0.0)
        bp, bm = jnp.maximum(b, 0.0), jnp.minimum(b, 0.0)
        for c in range(2):
            q = mt[c, l, 8:88, :]
            change = ap * (q - mt[c, l, 7:87, :]) + am * (mt[c, l, 9:89, :] - q)
            change = change + bp * (q - shifted(q, 1)) + bm * (shifted(q, -1) - q)
            ca[c, l, 8:88, :] = q - change

    for c in range(2):
        for l in range(4):
            q = ca[c, l, 8:88, :]
            total = ca[c, l, 7:87, :] + ca[c, l, 9:89, :]
            total = total + shifted(q, 1) + shifted(q, -1)
            total = total + ca[c, min(l + 1, 3), 8:88, :] + ca[c, max(l - 1, 0), 8:88, :]
            w1[c, l, 8:88, :] = (q + VISCOUS * total) * (1.0 / (1.0 + 6.0 * VISCOUS))
    for c in range(2):
        for l in range(4):
            q = w1[c, l, 16:80, :]
            total = w1[c, l, 15:79, 0:128] + w1[c, l, 17:81, 0:128]
            total = total + shifted(q, 1)[:, 0:128] + shifted(q, -1)[:, 0:128]
            total = total + w1[c, min(l + 1, 3), 16:80, 0:128] + w1[c, max(l - 1, 0), 16:80, 0:128]
            w2 = (ca[c, l, 16:80, 0:128] + VISCOUS * total) * (1.0 / (1.0 + 6.0 * VISCOUS))
            stage[l, c] = w2
            ta[c, 16:80, 128 * l : 128 * l + 128] = w2.astype(BF)

    out_copy = pltpu.make_async_copy(stage, out_v, out_sem)
    out_copy.start()

    lane64 = lax.broadcasted_iota(jnp.int32, (64, LANES), 1) // 16
    for side in range(2):
        packed = jnp.zeros((64, LANES), F32)
        for c in range(2):
            for l in range(4):
                spot = c * 4 + l
                shift = (spot * 16 - (112 if side == 0 else 0)) % LANES
                src = stage[l, c]
                moved = pltpu.roll(src, shift, 1) if shift else src
                packed = jnp.where(lane64 == spot, moved, packed)
        pks[side] = packed.astype(BF)
    second = []
    for n, (dx, dy) in enumerate(SIDES):
        if dy == 0:
            src, dst = (64, 0) if dx == 1 else (16, 80)
            second.append(
                send(n, ta.at[:, pl.ds(src, 16), :], ta.at[:, pl.ds(dst, 16), :], dx, dy, send2, recv2)
            )
            continue
        side = 0 if dy == 1 else 1
        if dx == 0:
            src, dst, size = 0, 16, 64
        elif dx == 1:
            src, dst, size = 48, 0, 16
        else:
            src, dst, size = 0, 80, 16
        second.append(
            send(n, pks.at[side, pl.ds(src, size)], rbs.at[side, pl.ds(dst, size)], dx, dy, send2, recv2)
        )
    for copy in second:
        copy.wait()

    below = rbs[0].astype(F32)
    above = rbs[1].astype(F32)
    tb[0] = jnp.where(low, below, pltpu.roll(above, 64, 1)).astype(BF)
    tb[1] = jnp.where(low, pltpu.roll(below, 64, 1), above).astype(BF)

    for r in range(4):
        lanes = slice(512 * r, 512 * r + 512)
        for c in range(2):
            part = jnp.dot(ta[c], wy_hot[0:512, lanes], preferred_element_type=F32)
            part = part + jnp.dot(tb[c], wy_hot[512:640, lanes], preferred_element_type=F32)
            summed = jnp.sum(part * wx_hot[:, lanes], axis=0, keepdims=True)
            for j in range(4):
                out_m[c, 4 * r + j : 4 * r + j + 1, :] = summed[:, LANES * j : LANES * j + LANES]
    out_copy.wait()


def body(velocity, marker_cell, marker_frac, marker_force, fish_owner):
    nx = lax.axis_size("gx")
    ny = lax.axis_size("gy")
    vm = pl.BlockSpec(memory_space=pltpu.VMEM)
    out_v, out_m = pl.pallas_call(
        functools.partial(kernel, nx, ny),
        out_shape=(
            jax.ShapeDtypeStruct((4, 2, 64, 128), F32),
            jax.ShapeDtypeStruct((2, 16, 128), F32),
        ),
        in_specs=[vm] * 5,
        out_specs=(pl.BlockSpec(memory_space=pl.ANY), vm),
        scratch_shapes=[
            pltpu.VMEM((23, 16, 128), F32),
            pltpu.VMEM((192, 2048), BF),
            pltpu.VMEM((96, 2048), F32),
            pltpu.VMEM((640, 2048), BF),
            pltpu.VMEM((2, 96, 640), F32),
            pltpu.VMEM((2, 96, 128), F32),
            pltpu.VMEM((2, 24, 128), F32),
            pltpu.VMEM((2, 2, 24, 640), F32),
            pltpu.VMEM((2, 80, 128), F32),
            pltpu.VMEM((2, 24, 128), F32),
            pltpu.VMEM((4, 24, 128), F32),
            pltpu.VMEM((4, 24, 128), F32),
            pltpu.VMEM((2, 4, 96, 256), F32),
            pltpu.VMEM((2, 4, 96, 256), F32),
            pltpu.VMEM((2, 4, 96, 256), F32),
            pltpu.VMEM((4, 2, 64, 128), F32),
            pltpu.VMEM((2, 96, 512), BF),
            pltpu.VMEM((2, 96, 128), BF),
            pltpu.VMEM((2, 64, 128), BF),
            pltpu.VMEM((2, 96, 128), BF),
            pltpu.SemaphoreType.DMA((16,)),
            pltpu.SemaphoreType.DMA((16,)),
            pltpu.SemaphoreType.DMA((8,)),
            pltpu.SemaphoreType.DMA((8,)),
            pltpu.SemaphoreType.DMA,
        ],
        compiler_params=pltpu.CompilerParams(
            collective_id=0, has_side_effects=True, vmem_limit_bytes=48 * 1024 * 1024
        ),
        name="fish_step",
    )(
        velocity,
        marker_cell.reshape(3, 16, 128),
        marker_frac.reshape(2, 16, 128),
        marker_force.reshape(2, 16, 128),
        fish_owner.reshape(6, 128),
    )
    return out_v, out_m.reshape(2, 1, 1, 2048)


def solution(mesh):
    placed = (
        P(None, None, "gx", "gy"),
        P(None, "gx", "gy", None),
        P(None, "gx", "gy", None),
        P(None, "gx", "gy", None),
        P(),
    )
    return jax.shard_map(
        body,
        mesh=mesh,
        in_specs=placed,
        out_specs=(P(None, None, "gx", "gy"), P(None, "gx", "gy", None)),
        check_vma=False,
    )
```

time: 132 us -> 34.7 us (0.26)
  the two profiles are of different devices: /device:TPU:60 before, /device:TPU:1 now
where the time goes in v1:
time: 34.7 us; the launch traced here: 34.4 us
  Pallas kernels  28.6 us (82%)
  local copies, waits for them, and re-layouts  5.11 us (15%)
  between operations  0.65 us (2%)
    pallas_call x1, Pallas kernels, body(): pl.pallas_call(functools.partial(kernel, nx, ny), out_shape=(jax.ShapeDty...  28.6 us
    unnamed x12, local copies, waits for them, and re-layouts  5.11 us

profile of v1, /device:TPU:1, one launch (start us, length us, event | category | flops | bytes accessed | tf_op | source)
XLA Modules:
  0.0 34.4 jit_solution(9974238219215258863)
XLA Ops:
  0.6 0.0 copy-start.4
  0.6 0.7 %copy-done.4 = s32[768]{0:T(1024)S(1)} copy-done((s32[768]{0:T(1024)S(1)}, s32[768]{0:T(1024)}, u32[]{:S(2)}) %copy-start.4) | copy-done | bytes 3096
  1.3 0.0 copy-start
  1.3 0.9 %copy-done = f32[4,2,64,128]{3,2,1,0:T(8,128)S(1)} copy-done((f32[4,2,64,128]{3,2,1,0:T(8,128)S(1)}, f32[4,2,64,128]{3,2,1,0:T(8,128)}, u32[]{:S(2)}) %copy-start) | copy-done | bytes 262168
  2.3 0.0 copy-start.1
  2.3 0.7 %copy-done.1 = s32[3,1,1,2048]{3,2,1,0:T(1,128)S(1)} copy-done((s32[3,1,1,2048]{3,2,1,0:T(1,128)S(1)}, s32[3,1,1,2048]{3,2,1,0:T(1,128)}, u32[]{:S(2)}) %copy-start.1) | copy-done | bytes 24600
  3.0 0.0 copy-start.2
  3.0 0.7 %copy-done.2 = f32[2,1,1,2048]{3,2,1,0:T(1,128)S(1)} copy-done((f32[2,1,1,2048]{3,2,1,0:T(1,128)S(1)}, f32[2,1,1,2048]{3,2,1,0:T(1,128)}, u32[]{:S(2)}) %copy-start.2) | copy-done | bytes 16408
  3.7 0.0 copy-start.3
  3.7 0.7 %copy-done.3 = f32[2,1,1,2048]{3,2,1,0:T(1,128)S(1)} copy-done((f32[2,1,1,2048]{3,2,1,0:T(1,128)S(1)}, f32[2,1,1,2048]{3,2,1,0:T(1,128)}, u32[]{:S(2)}) %copy-start.3) | copy-done | bytes 16408
  4.4 28.6 %fish_step.1 = (f32[4,2,64,128]{3,2,1,0:T(8,128)S(1)}, f32[2,16,128]{2,1,0:T(8,128)S(1)}) custom-call(f32[4,2,64,128]{3,2,1,0:T(8,128)S(1)} %copy-done, s32[3,16,128]{2,1,0:T(8,128)S(1)} %bitcast.5, f32[2,16,128]{2,1,0:T(8,128)S(1)} %bitcast.6, f32[2,16,128]{2,1,0:T(8,128)S(1)} %bitcast.7, s32[6,128]{1,0:T(8,128)S(1)} %bitcast.9), custom_call_target="tpu_custom_call" | custom-call | tf_op jit(solution)/shard_map/fish_step/pallas_call | solution.py:329
  33.0 0.7 %copy.10 = f32[4,2,64,128]{3,2,1,0:T(8,128)} copy(f32[4,2,64,128]{3,2,1,0:T(8,128)S(1)} %get-tuple-element.10) | data formatting | bytes 524288
  33.7 0.6 %copy.11 = f32[2,1,1,2048]{3,2,1,0:T(1,128)} copy(f32[2,1,1,2048]{3,2,1,0:T(1,128)S(1)} %bitcast.8) | data formatting | bytes 32768
Async XLA Ops:
  0.6 0.7 %copy-start.4 = (s32[768]{0:T(1024)S(1)}, s32[768]{0:T(1024)}, u32[]{:S(2)}) copy-start(s32[768]{0:T(1024)} %param.9) | copy-start | bytes 9220
  1.3 0.9 %copy-start = (f32[4,2,64,128]{3,2,1,0:T(8,128)S(1)}, f32[4,2,64,128]{3,2,1,0:T(8,128)}, u32[]{:S(2)}) copy-start(f32[4,2,64,128]{3,2,1,0:T(8,128)} %vel.1) | copy-start | bytes 786436
  2.3 0.7 %copy-start.1 = (s32[3,1,1,2048]{3,2,1,0:T(1,128)S(1)}, s32[3,1,1,2048]{3,2,1,0:T(1,128)}, u32[]{:S(2)}) copy-start(s32[3,1,1,2048]{3,2,1,0:T(1,128)} %param.6) | copy-start | bytes 73732
  3.0 0.7 %copy-start.2 = (f32[2,1,1,2048]{3,2,1,0:T(1,128)S(1)}, f32[2,1,1,2048]{3,2,1,0:T(1,128)}, u32[]{:S(2)}) copy-start(f32[2,1,1,2048]{3,2,1,0:T(1,128)} %param.7) | copy-start | bytes 49156
  3.7 0.7 %copy-start.3 = (f32[2,1,1,2048]{3,2,1,0:T(1,128)S(1)}, f32[2,1,1,2048]{3,2,1,0:T(1,128)}, u32[]{:S(2)}) copy-start(f32[2,1,1,2048]{3,2,1,0:T(1,128)} %param.8) | copy-start | bytes 49156

commit v2 on v1

v2 whole, which is shorter than its diff:
```python
import functools
import math

import jax
import jax.numpy as jnp
from jax import lax
from jax.experimental import pallas as pl
from jax.experimental.pallas import tpu as pltpu
from jax.sharding import PartitionSpec as P

MARGIN = 16
FISH_MARK = 1024
COURANT = 0.25
VISCOUS = 1.5
LANES = 128
BF = jnp.bfloat16
F32 = jnp.float32

SIDES = [(1, 0), (-1, 0), (0, 1), (0, -1), (1, 1), (-1, 1), (1, -1), (-1, -1)]


def half_angle(t):
    z = t * (0.5 * math.pi)
    q = z * z
    s = 1.0 / math.factorial(13)
    for n in (11, 9, 7, 5, 3, 1):
        s = s * q + (-1.0) ** ((n - 1) // 2) / math.factorial(n)
    c = 1.0 / math.factorial(12)
    for n in (10, 8, 6, 4, 2, 0):
        c = c * q + (-1.0) ** (n // 2) / math.factorial(n)
    return s * z, c


def weights(t):
    s, c = half_angle(t)
    return (0.25 * (1.0 - s), 0.25 * (1.0 + c), 0.25 * (1.0 + s), 0.25 * (1.0 - c))


def chain(d, values, zero):
    out = jnp.where(d == 2.0, values[3], zero)
    out = jnp.where(d == 1.0, values[2], out)
    out = jnp.where(d == 0.0, values[1], out)
    return jnp.where(d == -1.0, values[0], out)


def kernel(
    nx, ny,
    vel_h, cell_h, frac_h, force_h, owner_h,
    out_v, out_m,
    vel, cell, frac, force, owner,
    q32, left, wx_hot, wy_hot, mv, pk16, pko, rx, ry16, ryo, rc16, rco,
    mt, ca, w1, ta,
    in_sem, send1, recv1,
):
    ix = lax.axis_index("gx")
    iy = lax.axis_index("gy")

    def at(dx, dy):
        return {"gx": lax.rem(ix + dx + nx, nx), "gy": lax.rem(iy + dy + ny, ny)}

    barrier = pltpu.get_barrier_semaphore()
    for dx, dy in SIDES:
        pl.semaphore_signal(
            barrier, inc=1, device_id=at(dx, dy), device_id_type=pl.DeviceIdType.MESH
        )
    loads = []
    for n, (src, dst) in enumerate(
        ((cell_h, cell), (frac_h, frac), (force_h, force), (owner_h, owner), (vel_h, vel))
    ):
        loads.append(pltpu.make_async_copy(src, dst, in_sem.at[n]))
        loads[-1].start()
    for load in loads[:4]:
        load.wait()

    mine = jnp.where(owner[...] == ix * ny + iy, 1.0, 0.0)
    count = jnp.sum(jnp.sum(mine, axis=1, keepdims=True), axis=0, keepdims=True)
    slot = lax.broadcasted_iota(jnp.int32, (16, LANES), 0) * LANES + lax.broadcasted_iota(
        jnp.int32, (16, LANES), 1
    )
    alive = jnp.where(slot.astype(F32) < FISH_MARK * count, 1.0, 0.0)
    rel_x = lax.rem(cell[0] - ix * 64 + (MARGIN + nx * 64), nx * 64)
    rel_y = lax.rem(cell[1] - iy * 128 + (MARGIN + ny * 128), ny * 128) - MARGIN
    q32[0] = rel_x.astype(F32)
    q32[1] = rel_y.astype(F32)
    wx = weights(frac[0])
    wy = weights(frac[1])
    for k in range(4):
        q32[2 + k] = wx[k]
        q32[6 + k] = wy[k]
        for c in range(2):
            q32[10 + 4 * c + k] = force[c] * alive * wx[k]
        q32[18 + k] = jnp.where(cell[2] == k, 1.0, 0.0)
    q32[22] = alive

    rows16 = lax.broadcasted_iota(jnp.int32, (16, LANES), 0).astype(F32)
    zero16 = jnp.zeros((16, LANES), BF)
    strips = ((512, -26.0), (528, -10.0), (640, 122.0), (656, 138.0))

    def operands(r, _):
        lanes = pl.ds(pl.multiple_of(r * LANES, LANES), LANES)

        def row(n):
            return jnp.broadcast_to(q32[n, pl.ds(r, 1), :], (16, LANES))

        dx0 = rows16 - row(0)
        lw = [[row(10 + 4 * c + k).astype(BF) for k in range(4)] for c in range(2)]
        for b in range(6):
            d = (dx0 + 16.0 * b).astype(BF)
            for c in range(2):
                left[pl.ds(96 * c + 16 * b, 16), lanes] = chain(d, lw[c], zero16)
        dy0 = rows16 - row(1)
        yw = [row(6 + k).astype(BF) for k in range(4)]
        lv = [row(18 + k).astype(BF) for k in range(4)]
        for b in range(12):
            base, step = (16.0 * b, 128) if b < 8 else (strips[b - 8][1], 32)
            first_row = 16 * b if b < 8 else strips[b - 8][0]
            d = (dy0 + base).astype(BF)
            w = chain(d, yw, zero16)
            for l in range(4):
                wy_hot[pl.ds(first_row + step * l, 16), lanes] = w * lv[l]
        return 0

    lax.fori_loop(0, 16, operands, 0)

    loads[4].wait()
    lane64 = lax.broadcasted_iota(jnp.int32, (64, LANES), 1)
    level64, j64 = lane64 // 32, lane64 % 32
    for c in range(2):
        spread = lax.dot_general(
            left[pl.ds(96 * c, 96), :], wy_hot[...], (((1,), (1,)), ((), ())),
            preferred_element_type=F32,
        )
        mv[c] = spread
        low_part = jnp.zeros((64, LANES), F32)
        high_part = jnp.zeros((64, LANES), F32)
        for l in range(4):
            ls = slice(128 * l, 128 * l + 128)
            v = vel[l, c]
            mv[c, 16:80, ls] = spread[16:80, ls] + v
            low_part = jnp.where(
                (level64 == l) & (j64 >= 26), pltpu.roll(v, 32 * l + 26, 1), low_part
            )
            high_part = jnp.where(
                (level64 == l) & (j64 < 6), pltpu.roll(v, 32 * l + 6, 1), high_part
            )
        mv[c, 16:80, 512:640] = spread[16:80, 512:640] + low_part
        mv[c, 16:80, 640:768] = spread[16:80, 640:768] + high_part

    lane = lax.broadcasted_iota(jnp.int32, (96, LANES), 1)
    level, j = lane // 32, lane % 32
    strip0 = [mv[c, :, 512:640] for c in range(2)]
    strip1 = [mv[c, :, 640:768] for c in range(2)]
    near = j < 16
    pk16[0] = jnp.where(near, pltpu.roll(strip1[0], 122, 1), pltpu.roll(strip1[1], 10, 1)).astype(BF)
    pk16[1] = jnp.where(near, pltpu.roll(strip0[0], 118, 1), pltpu.roll(strip0[1], 6, 1)).astype(BF)
    for c in range(2):
        up = pltpu.roll(strip1[c], 20, 1)
        down = pltpu.roll(strip0[c], 108, 1)
        for l in range(4):
            t = mv[c, :, 128 * l : 128 * l + 128]
            up = jnp.where((level == l) & (j < 26), pltpu.roll(t, (32 * l + 26) % LANES, 1), up)
            down = jnp.where((level == l) & (j >= 6), pltpu.roll(t, 32 * l + 6, 1), down)
        pko[0, c] = up
        pko[1, c] = down

    pl.semaphore_wait(barrier, 8)

    copies = []

    def send(n, src, dst, dx, dy):
        copy = pltpu.make_async_remote_copy(
            src_ref=src, dst_ref=dst, send_sem=send1.at[n], recv_sem=recv1.at[n],
            device_id=at(dx, dy), device_id_type=pl.DeviceIdType.MESH,
        )
        copy.start()
        copies.append(copy)

    for n, (dx, dy) in enumerate(SIDES):
        if dy == 0:
            continue
        side = 0 if dy == 1 else 1
        if dx == 0:
            send(2 * n, pko.at[side], ryo.at[side], dx, dy)
            send(2 * n + 1, pk16.at[side], ry16.at[side], dx, dy)
        else:
            send(2 * n, pko.at[side, :, pl.ds(56 if dx == 1 else 0, 40)], rco.at[n - 4], dx, dy)
            send(2 * n + 1, pk16.at[side, pl.ds(48 if dx == 1 else 0, 48)], rc16.at[n - 4], dx, dy)
    send(0, mv.at[:, pl.ds(56, 40), :], rx.at[0], 1, 0)
    send(2, mv.at[:, pl.ds(0, 40), :], rx.at[1], -1, 0)

    rows8 = lax.broadcasted_iota(jnp.int32, (8, LANES), 0).astype(F32)

    def x_hot(r, _):
        lanes = pl.ds(pl.multiple_of(r * LANES, LANES), LANES)

        def row(n):
            return jnp.broadcast_to(q32[n, pl.ds(r, 1), :], (8, LANES))

        d = rows8 - row(0)
        ww = [row(2 + k) * row(22) for k in range(4)]
        for b in range(12):
            wx_hot[pl.ds(8 * b, 8), lanes] = chain(d + 8.0 * b, ww, 0.0)
        return 0

    lax.fori_loop(0, 16, x_hot, 0)
    for ref in (mt, ca, w1):
        for c in range(2):
            for t in range(6):
                ref[c, t, 0:8, :] = jnp.zeros((8, LANES), F32)
                ref[c, t, 120:128, :] = jnp.zeros((8, LANES), F32)

    for copy in copies:
        copy.wait()

    corner = {}
    for n in range(4):
        dx, dy = SIDES[4 + n]
        corner[0 if dx == 1 else 1, 0 if dy == 1 else 1] = n

    def joined(mid, first, last):
        return [
            first[0:8], mid[0:32] + first[8:40], mid[32:64], mid[64:96] + last[0:32], last[32:40]
        ]

    pack16 = [
        jnp.concatenate(
            joined(
                ry16[side].astype(F32),
                rc16[corner[0, side]].astype(F32)[8:48],
                rc16[corner[1, side]].astype(F32)[0:40],
            ),
            axis=0,
        )
        for side in range(2)
    ]
    lane112 = lax.broadcasted_iota(jnp.int32, (112, LANES), 1)

    def rolled(q, by):
        return pltpu.roll(q, by % LANES, 1) if by % LANES else q

    for c in range(2):
        for t in range(6):
            ls = slice(128 * t, 128 * t + 128)
            mid, first, last = mv[c, :, ls], rx[0, c, :, ls], rx[1, c, :, ls]
            if t < 4:
                a = jnp.concatenate(joined(mid, first, last), axis=0)
                g = 32 * t + 16 * c
                a = a + jnp.where(lane112 < 16, rolled(pack16[0], -g), 0.0)
                a = a + jnp.where(lane112 >= 112, rolled(pack16[1], 112 - g), 0.0)
            else:
                side = t - 4
                mid = mid + ryo[side, c]
                first = first + rco[corner[0, side], c]
                last = last + rco[corner[1, side], c]
                a = jnp.concatenate(joined(mid, first, last), axis=0)
            mt[c, t, 8:120, :] = a

    for t in range(6):
        a = COURANT * mt[0, t, 8:120, :]
        b = COURANT * mt[1, t, 8:120, :]
        ap, am = jnp.maximum(a, 0.0), jnp.minimum(a, 0.0)
        bp, bm = jnp.maximum(b, 0.0), jnp.minimum(b, 0.0)
        for c in range(2):
            q = mt[c, t, 8:120, :]
            change = ap * (q - mt[c, t, 7:119, :]) + am * (mt[c, t, 9:121, :] - q)
            change = change + bp * (q - rolled(q, 1)) + bm * (rolled(q, -1) - q)
            ca[c, t, 8:120, :] = q - change

    def around(ref, c, t, lo, hi):
        q = ref[c, t, lo:hi, :]
        total = ref[c, t, lo - 1 : hi - 1, :] + ref[c, t, lo + 1 : hi + 1, :]
        total = total + rolled(q, 1) + rolled(q, -1)
        if t < 4:
            return total + ref[c, min(t + 1, 3), lo:hi, :] + ref[c, max(t - 1, 0), lo:hi, :]
        lanes = lax.broadcasted_iota(jnp.int32, (hi - lo, LANES), 1)
        total = total + jnp.where(lanes >= 96, q, rolled(q, -32))
        return total + jnp.where(lanes < 32, q, rolled(q, 32))

    scale = 1.0 / (1.0 + 6.0 * VISCOUS)
    for c in range(2):
        for t in range(6):
            w1[c, t, 8:120, :] = (ca[c, t, 8:120, :] + VISCOUS * around(ca, c, t, 8, 120)) * scale
    for c in range(2):
        done = [
            (ca[c, t, 16:112, :] + VISCOUS * around(w1, c, t, 16, 112)) * scale for t in (4, 5)
        ]
        for l in range(4):
            w2 = (ca[c, l, 16:112, :] + VISCOUS * around(w1, c, l, 16, 112)) * scale
            w2 = jnp.where(lane < 3, rolled(done[0], -(32 * l + 26)), w2)
            w2 = jnp.where(lane >= 125, rolled(done[1], 122 - 32 * l), w2)
            out_v[l, c] = w2[16:80]
            ta[c, :, 128 * l : 128 * l + 128] = w2.astype(BF)
        ta[c, :, 512:640] = jnp.where((j >= 10) & (j < 26), done[0], 0.0).astype(BF)
        ta[c, :, 640:768] = jnp.where((j >= 6) & (j < 22), done[1], 0.0).astype(BF)

    for r in range(4):
        lanes = slice(512 * r, 512 * r + 512)
        for c in range(2):
            part = jnp.dot(ta[c], wy_hot[:, lanes], preferred_element_type=F32)
            summed = jnp.sum(part * wx_hot[:, lanes], axis=0, keepdims=True)
            for i in range(4):
                out_m[c, 4 * r + i : 4 * r + i + 1, :] = summed[:, LANES * i : LANES * i + LANES]


def body(velocity, marker_cell, marker_frac, marker_force, fish_owner):
    nx = lax.axis_size("gx")
    ny = lax.axis_size("gy")
    vm = pl.BlockSpec(memory_space=pltpu.VMEM)
    out_v, out_m = pl.pallas_call(
        functools.partial(kernel, nx, ny),
        out_shape=(
            jax.ShapeDtypeStruct((4, 2, 64, 128), F32),
            jax.ShapeDtypeStruct((2, 16, 128), F32),
        ),
        in_specs=[pl.BlockSpec(memory_space=pltpu.HBM)] * 5,
        out_specs=(vm, vm),
        scratch_shapes=[
            pltpu.VMEM((4, 2, 64, 128), F32),
            pltpu.VMEM((3, 16, 128), jnp.int32),
            pltpu.VMEM((2, 16, 128), F32),
            pltpu.VMEM((2, 16, 128), F32),
            pltpu.VMEM((6, 128), jnp.int32),
            pltpu.VMEM((23, 16, 128), F32),
            pltpu.VMEM((192, 2048), BF),
            pltpu.VMEM((96, 2048), F32),
            pltpu.VMEM((768, 2048), BF),
            pltpu.VMEM((2, 96, 768), F32),
            pltpu.VMEM((2, 96, 128), BF),
            pltpu.VMEM((2, 2, 96, 128), F32),
            pltpu.VMEM((2, 2, 40, 768), F32),
            pltpu.VMEM((2, 96, 128), BF),
            pltpu.VMEM((2, 2, 96, 128), F32),
            pltpu.VMEM((4, 48, 128), BF),
            pltpu.VMEM((4, 2, 40, 128), F32),
            pltpu.VMEM((2, 6, 128, 128), F32),
            pltpu.VMEM((2, 6, 128, 128), F32),
            pltpu.VMEM((2, 6, 128, 128), F32),
            pltpu.VMEM((2, 96, 768), BF),
            pltpu.SemaphoreType.DMA((5,)),
            pltpu.SemaphoreType.DMA((16,)),
            pltpu.SemaphoreType.DMA((16,)),
        ],
        compiler_params=pltpu.CompilerParams(
            collective_id=0, has_side_effects=True, vmem_limit_bytes=32 * 1024 * 1024
        ),
        name="fish_step",
    )(
        velocity,
        marker_cell.reshape(3, 16, 128),
        marker_frac.reshape(2, 16, 128),
        marker_force.reshape(2, 16, 128),
        fish_owner.reshape(6, 128),
    )
    return out_v, out_m.reshape(2, 1, 1, 2048)


def solution(mesh):
    placed = (
        P(None, None, "gx", "gy"),
        P(None, "gx", "gy", None),
        P(None, "gx", "gy", None),
        P(None, "gx", "gy", None),
        P(),
    )
    return jax.shard_map(
        body,
        mesh=mesh,
        in_specs=placed,
        out_specs=(P(None, None, "gx", "gy"), P(None, "gx", "gy", None)),
        check_vma=False,
    )
```

time: 34.7 us -> 32.4 us (0.934)
  Pallas kernels: 28.6 us -> 26.3 us
    pallas_call x1, Pallas kernels: 28.6 us -> 26.3 us  [body(): pl.pallas_call(functools.partial(kernel, nx, ny), out_shape=(jax.ShapeDty...]
where the time goes in v2:
time: 32.4 us; the launch traced here: 32.1 us
  Pallas kernels  26.3 us (81%)
  local copies, waits for them, and re-layouts  5.11 us (16%)
  between operations  0.65 us (2%)
    pallas_call x1, Pallas kernels, body(): pl.pallas_call(functools.partial(kernel, nx, ny), out_shape=(jax.ShapeDty...  26.3 us
    unnamed x12, local copies, waits for them, and re-layouts  5.11 us

profile of v2, /device:TPU:1, one launch (start us, length us, event | category | flops | bytes accessed | tf_op | source)
XLA Modules:
  0.0 32.1 jit_solution(13085173426320998366)
XLA Ops:
  0.6 0.0 copy-start.4
  0.6 0.7 %copy-done.4 = s32[768]{0:T(1024)S(1)} copy-done((s32[768]{0:T(1024)S(1)}, s32[768]{0:T(1024)}, u32[]{:S(2)}) %copy-start.4) | copy-done | bytes 3096
  1.3 0.0 copy-start
  1.3 0.9 %copy-done = f32[4,2,64,128]{3,2,1,0:T(8,128)S(1)} copy-done((f32[4,2,64,128]{3,2,1,0:T(8,128)S(1)}, f32[4,2,64,128]{3,2,1,0:T(8,128)}, u32[]{:S(2)}) %copy-start) | copy-done | bytes 262168
  2.3 0.0 copy-start.1
  2.3 0.7 %copy-done.1 = s32[3,1,1,2048]{3,2,1,0:T(1,128)S(1)} copy-done((s32[3,1,1,2048]{3,2,1,0:T(1,128)S(1)}, s32[3,1,1,2048]{3,2,1,0:T(1,128)}, u32[]{:S(2)}) %copy-start.1) | copy-done | bytes 24600
  3.0 0.0 copy-start.2
  3.0 0.7 %copy-done.2 = f32[2,1,1,2048]{3,2,1,0:T(1,128)S(1)} copy-done((f32[2,1,1,2048]{3,2,1,0:T(1,128)S(1)}, f32[2,1,1,2048]{3,2,1,0:T(1,128)}, u32[]{:S(2)}) %copy-start.2) | copy-done | bytes 16408
  3.7 0.0 copy-start.3
  3.7 0.7 %copy-done.3 = f32[2,1,1,2048]{3,2,1,0:T(1,128)S(1)} copy-done((f32[2,1,1,2048]{3,2,1,0:T(1,128)S(1)}, f32[2,1,1,2048]{3,2,1,0:T(1,128)}, u32[]{:S(2)}) %copy-start.3) | copy-done | bytes 16408
  4.4 26.3 %fish_step.1 = (f32[4,2,64,128]{3,2,1,0:T(8,128)S(1)}, f32[2,16,128]{2,1,0:T(8,128)S(1)}) custom-call(f32[4,2,64,128]{3,2,1,0:T(8,128)S(1)} %copy-done, s32[3,16,128]{2,1,0:T(8,128)S(1)} %bitcast.5, f32[2,16,128]{2,1,0:T(8,128)S(1)} %bitcast.6, f32[2,16,128]{2,1,0:T(8,128)S(1)} %bitcast.7, s32[6,128]{1,0:T(8,128)S(1)} %bitcast.9), custom_call_target="tpu_custom_call" | custom-call | tf_op jit(solution)/shard_map/fish_step/pallas_call | solution.py:309
  30.8 0.7 %copy.10 = f32[4,2,64,128]{3,2,1,0:T(8,128)} copy(f32[4,2,64,128]{3,2,1,0:T(8,128)S(1)} %get-tuple-element.10) | data formatting | bytes 524288
  31.5 0.6 %copy.11 = f32[2,1,1,2048]{3,2,1,0:T(1,128)} copy(f32[2,1,1,2048]{3,2,1,0:T(1,128)S(1)} %bitcast.8) | data formatting | bytes 32768
Async XLA Ops:
  0.6 0.7 %copy-start.4 = (s32[768]{0:T(1024)S(1)}, s32[768]{0:T(1024)}, u32[]{:S(2)}) copy-start(s32[768]{0:T(1024)} %param.9) | copy-start | bytes 9220
  1.3 0.9 %copy-start = (f32[4,2,64,128]{3,2,1,0:T(8,128)S(1)}, f32[4,2,64,128]{3,2,1,0:T(8,128)}, u32[]{:S(2)}) copy-start(f32[4,2,64,128]{3,2,1,0:T(8,128)} %vel_h.1) | copy-start | bytes 786436
  2.3 0.7 %copy-start.1 = (s32[3,1,1,2048]{3,2,1,0:T(1,128)S(1)}, s32[3,1,1,2048]{3,2,1,0:T(1,128)}, u32[]{:S(2)}) copy-start(s32[3,1,1,2048]{3,2,1,0:T(1,128)} %param.6) | copy-start | bytes 73732
  3.0 0.7 %copy-start.2 = (f32[2,1,1,2048]{3,2,1,0:T(1,128)S(1)}, f32[2,1,1,2048]{3,2,1,0:T(1,128)}, u32[]{:S(2)}) copy-start(f32[2,1,1,2048]{3,2,1,0:T(1,128)} %param.7) | copy-start | bytes 49156
  3.7 0.7 %copy-start.3 = (f32[2,1,1,2048]{3,2,1,0:T(1,128)S(1)}, f32[2,1,1,2048]{3,2,1,0:T(1,128)}, u32[]{:S(2)}) copy-start(f32[2,1,1,2048]{3,2,1,0:T(1,128)} %param.8) | copy-start | bytes 49156

commit v3 on v2

--- a/solution.py
+++ b/solution.py
@@ -48,7 +48,7 @@
     vel_h, cell_h, frac_h, force_h, owner_h,
     out_v, out_m,
     vel, cell, frac, force, owner,
-    q32, left, wx_hot, wy_hot, mv, pk16, pko, rx, ry16, ryo, rc16, rco,
+    q32, left, wx_hot, wy_hot, mv, px, py, pc, rx, ry, rc,
     mt, ca, w1, ta,
     in_sem, send1, recv1,
 ):
@@ -151,8 +151,11 @@
     strip0 = [mv[c, :, 512:640] for c in range(2)]
     strip1 = [mv[c, :, 640:768] for c in range(2)]
     near = j < 16
-    pk16[0] = jnp.where(near, pltpu.roll(strip1[0], 122, 1), pltpu.roll(strip1[1], 10, 1)).astype(BF)
-    pk16[1] = jnp.where(near, pltpu.roll(strip0[0], 118, 1), pltpu.roll(strip0[1], 6, 1)).astype(BF)
+    outer = [
+        jnp.where(near, pltpu.roll(strip1[0], 122, 1), pltpu.roll(strip1[1], 10, 1)),
+        jnp.where(near, pltpu.roll(strip0[0], 118, 1), pltpu.roll(strip0[1], 6, 1)),
+    ]
+    inner = [[], []]
     for c in range(2):
         up = pltpu.roll(strip1[c], 20, 1)
         down = pltpu.roll(strip0[c], 108, 1)
@@ -160,8 +163,19 @@
             t = mv[c, :, 128 * l : 128 * l + 128]
             up = jnp.where((level == l) & (j < 26), pltpu.roll(t, (32 * l + 26) % LANES, 1), up)
             down = jnp.where((level == l) & (j >= 6), pltpu.roll(t, 32 * l + 6, 1), down)
-        pko[0, c] = up
-        pko[1, c] = down
+        inner[0].append(up)
+        inner[1].append(down)
+    filler = jnp.zeros((8, LANES), F32)
+    for side in range(2):
+        parts = [inner[side][0], inner[side][1], outer[side]]
+        py[side] = jnp.concatenate(parts, axis=0).astype(BF)
+        for n in range(4):
+            dx, dy = SIDES[4 + n]
+            if (0 if dy == 1 else 1) == side:
+                lo = 56 if dx == 1 else 0
+                pc[n] = jnp.concatenate([p[lo : lo + 40] for p in parts] + [filler], axis=0).astype(BF)
+    for n, lo in enumerate((56, 0)):
+        px[n] = jnp.concatenate([mv[0, lo : lo + 40, :], mv[1, lo : lo + 40, :]], axis=0).astype(BF)
 
     pl.semaphore_wait(barrier, 8)
 
@@ -175,18 +189,12 @@
         copy.start()
         copies.append(copy)
 
-    for n, (dx, dy) in enumerate(SIDES):
-        if dy == 0:
-            continue
-        side = 0 if dy == 1 else 1
-        if dx == 0:
-            send(2 * n, pko.at[side], ryo.at[side], dx, dy)
-            send(2 * n + 1, pk16.at[side], ry16.at[side], dx, dy)
-        else:
-            send(2 * n, pko.at[side, :, pl.ds(56 if dx == 1 else 0, 40)], rco.at[n - 4], dx, dy)
-            send(2 * n + 1, pk16.at[side, pl.ds(48 if dx == 1 else 0, 48)], rc16.at[n - 4], dx, dy)
-    send(0, mv.at[:, pl.ds(56, 40), :], rx.at[0], 1, 0)
-    send(2, mv.at[:, pl.ds(0, 40), :], rx.at[1], -1, 0)
+    for n in range(4):
+        send(4 + n, pc.at[n], rc.at[n], *SIDES[4 + n])
+    for n in range(2):
+        send(2 + n, py.at[n], ry.at[n], *SIDES[2 + n])
+    for n in range(2):
+        send(n, px.at[n], rx.at[n], *SIDES[n])
 
     rows8 = lax.broadcasted_iota(jnp.int32, (8, LANES), 0).astype(F32)
 
@@ -222,14 +230,14 @@
             first[0:8], mid[0:32] + first[8:40], mid[32:64], mid[64:96] + last[0:32], last[32:40]
         ]
 
+    ryf = [ry[side].astype(F32) for side in range(2)]
+    rcf = [rc[n].astype(F32) for n in range(4)]
+    rxf = [rx[n].astype(F32) for n in range(2)]
+    from_y = [[r[96 * p : 96 * p + 96] for p in range(3)] for r in ryf]
+    from_c = [[r[40 * p : 40 * p + 40] for p in range(3)] for r in rcf]
     pack16 = [
         jnp.concatenate(
-            joined(
-                ry16[side].astype(F32),
-                rc16[corner[0, side]].astype(F32)[8:48],
-                rc16[corner[1, side]].astype(F32)[0:40],
-            ),
-            axis=0,
+            joined(from_y[side][2], from_c[corner[0, side]][2], from_c[corner[1, side]][2]), axis=0
         )
         for side in range(2)
     ]
@@ -241,7 +249,8 @@
     for c in range(2):
         for t in range(6):
             ls = slice(128 * t, 128 * t + 128)
-            mid, first, last = mv[c, :, ls], rx[0, c, :, ls], rx[1, c, :, ls]
+            mid = mv[c, :, ls]
+            first, last = (r[40 * c : 40 * c + 40, ls] for r in rxf)
             if t < 4:
                 a = jnp.concatenate(joined(mid, first, last), axis=0)
                 g = 32 * t + 16 * c
@@ -249,9 +258,9 @@
                 a = a + jnp.where(lane112 >= 112, rolled(pack16[1], 112 - g), 0.0)
             else:
                 side = t - 4
-                mid = mid + ryo[side, c]
-                first = first + rco[corner[0, side], c]
-                last = last + rco[corner[1, side], c]
+                mid = mid + from_y[side][c]
+                first = first + from_c[corner[0, side]][c]
+                last = last + from_c[corner[1, side]][c]
                 a = jnp.concatenate(joined(mid, first, last), axis=0)
             mt[c, t, 8:120, :] = a
 
@@ -325,31 +334,30 @@
             pltpu.VMEM((96, 2048), F32),
             pltpu.VMEM((768, 2048), BF),
             pltpu.VMEM((2, 96, 768), F32),
-            pltpu.VMEM((2, 96, 128), BF),
-            pltpu.VMEM((2, 2, 96, 128), F32),
-            pltpu.VMEM((2, 2, 40, 768), F32),
-            pltpu.VMEM((2, 96, 128), BF),
-            pltpu.VMEM((2, 2, 96, 128), F32),
-            pltpu.VMEM((4, 48, 128), BF),
-            pltpu.VMEM((4, 2, 40, 128), F32),
+            pltpu.VMEM((2, 80, 768), BF),
+            pltpu.VMEM((2, 288, 128), BF),
+            pltpu.VMEM((4, 128, 128), BF),
+            pltpu.VMEM((2, 80, 768), BF),
+            pltpu.VMEM((2, 288, 128), BF),
+            pltpu.VMEM((4, 128, 128), BF),
             pltpu.VMEM((2, 6, 128, 128), F32),
             pltpu.VMEM((2, 6, 128, 128), F32),
             pltpu.VMEM((2, 6, 128, 128), F32),
             pltpu.VMEM((2, 96, 768), BF),
             pltpu.SemaphoreType.DMA((5,)),
-            pltpu.SemaphoreType.DMA((16,)),
-            pltpu.SemaphoreType.DMA((16,)),
+            pltpu.SemaphoreType.DMA((8,)),
+            pltpu.SemaphoreType.DMA((8,)),
         ],
         compiler_params=pltpu.CompilerParams(
             collective_id=0, has_side_effects=True, vmem_limit_bytes=32 * 1024 * 1024
         ),
         name="fish_step",
     )(
-        velocity,
-        marker_cell.reshape(3, 16, 128),
-        marker_frac.reshape(2, 16, 128),
-        marker_force.reshape(2, 16, 128),
-        fish_owner.reshape(6, 128),
+        pltpu.with_memory_space_constraint(velocity, pltpu.HBM),
+        pltpu.with_memory_space_constraint(marker_cell.reshape(3, 16, 128), pltpu.HBM),
+        pltpu.with_memory_space_constraint(marker_frac.reshape(2, 16, 128), pltpu.HBM),
+        pltpu.with_memory_space_constraint(marker_force.reshape(2, 16, 128), pltpu.HBM),
+        pltpu.with_memory_space_constraint(fish_owner.reshape(6, 128), pltpu.HBM),
     )
     return out_v, out_m.reshape(2, 1, 1, 2048)
 

time: 32.4 us -> 23.4 us (0.72)
  the two profiles are of different devices: /device:TPU:1 before, /device:TPU:56 now
where the time goes in v3:
time: 23.4 us; the launch traced here: 23 us
  Pallas kernels  21.1 us (90%)
  local copies, waits for them, and re-layouts  1.31 us (6%)
  between operations  0.64 us (3%)
    pallas_call x1, Pallas kernels, body(): pl.pallas_call(functools.partial(kernel, nx, ny), out_shape=(jax.ShapeDty...  21.1 us
    unnamed x2, local copies, waits for them, and re-layouts  1.31 us

profile of v3, /device:TPU:56, one launch (start us, length us, event | category | flops | bytes accessed | tf_op | source)
XLA Modules:
  0.0 23.0 jit_solution(13977745812803890769)
XLA Ops:
  0.6 21.1 %fish_step.1 = (f32[4,2,64,128]{3,2,1,0:T(8,128)S(1)}, f32[2,16,128]{2,1,0:T(8,128)S(1)}) custom-call(f32[4,2,64,128]{3,2,1,0:T(8,128)} %vel_h.1, s32[3,16,128]{2,1,0:T(8,128)} %bitcast.6, f32[2,16,128]{2,1,0:T(8,128)} %bitcast.7, f32[2,16,128]{2,1,0:T(8,128)} %bitcast.8, s32[6,128]{1,0:T(8,128)} %bitcast.9), custom_call_target="tpu_custom_call" | custom-call | tf_op jit(solution)/shard_map/fish_step/pallas_call | solution.py:318
  21.7 0.7 %copy.10 = f32[4,2,64,128]{3,2,1,0:T(8,128)} copy(f32[4,2,64,128]{3,2,1,0:T(8,128)S(1)} %get-tuple-element.10) | data formatting | bytes 524288
  22.4 0.6 %copy.11 = f32[2,1,1,2048]{3,2,1,0:T(1,128)} copy(f32[2,1,1,2048]{3,2,1,0:T(1,128)S(1)} %bitcast.5) | data formatting | bytes 32768

commit v4 on v3

--- a/solution.py
+++ b/solution.py
@@ -43,13 +43,69 @@
     return jnp.where(d == -1.0, values[0], out)
 
 
+def pick(ref, source):
+    rows, columns = ref.shape
+    n = lax.broadcasted_iota(jnp.int32, (16, columns), 1)
+    below = source(n) - lax.broadcasted_iota(jnp.int32, (16, columns), 0)
+    for lo in range(0, rows, 16):
+        ref[lo : lo + 16, :] = jnp.where(below == lo, 1.0, 0.0).astype(BF)
+
+
+def matrices(w_in, w_out, w_place, w_adv, w_t, w_s, w_fix):
+    def inner_of(n):
+        p, l = n % 32, (n // 32) % 4
+        up = jnp.where(p < 26, 128 * l + p + 102, 640 + 32 * l + p - 20)
+        down = jnp.where(p < 6, 512 + 32 * l + p + 20, 128 * l + p - 6)
+        return jnp.where(n < 128, up, down)
+
+    def outer_of(n):
+        i, c, l = n % 16, (n // 16) % 2, (n // 32) % 4
+        return 256 * c + 32 * l + i + jnp.where(n < 128, 128 + 6, 10)
+
+    def place_of(n):
+        y, l, c = n % 128, (n // 128) % 4, n // 512
+        at = 32 * l + 16 * c
+        return jnp.where(y < 16, at + y, jnp.where(y >= 112, 128 + at + y - 112, -1))
+
+    def fix_of(n):
+        y, l = n % 128, n // 128
+        return jnp.where(
+            y < 3, 32 * l + 26 + y, jnp.where(y >= 125, 128 + 32 * l + y - 122, -1)
+        )
+
+    pick(w_in, inner_of)
+    pick(w_out, outer_of)
+    pick(w_place, place_of)
+    pick(w_fix, fix_of)
+    y = lax.broadcasted_iota(jnp.int32, (16, LANES), 1)
+    r = lax.broadcasted_iota(jnp.int32, (16, LANES), 0)
+
+    def one(of):
+        return jnp.where(of == r, 1.0, 0.0)
+
+    for lo in range(0, 256, 16):
+        base = lo % LANES
+        here, prev, after = one(y - base), one((y + 127) % 128 - base), one((y + 1) % 128 - base)
+        w_adv[lo : lo + 16, 0:128] = (here - prev).astype(BF)
+        w_adv[lo : lo + 16, 128:256] = (after - here).astype(BF)
+        w_t[lo : lo + 16, :] = (prev + after).astype(BF)
+        upper = one(jnp.where(y < 96, y + 32, y) - base)
+        lower = one(jnp.where(y >= 32, y - 32, y) - base)
+        w_s[lo : lo + 16, :] = (prev + after + upper + lower).astype(BF)
+
+
+def pieces(v):
+    high = v.astype(BF)
+    return high, (v - high.astype(F32)).astype(BF)
+
+
 def kernel(
     nx, ny,
     vel_h, cell_h, frac_h, force_h, owner_h,
     out_v, out_m,
     vel, cell, frac, force, owner,
-    q32, left, wx_hot, wy_hot, mv, px, py, pc, rx, ry, rc,
-    mt, ca, w1, ta,
+    q32, left, wx_hot, wy_hot, mv, mvb, px, py, pc, rx, ry, rc,
+    mt, ca, w1, sp, ws, ta, w_in, w_out, w_place, w_adv, w_t, w_s, w_fix,
     in_sem, send1, recv1,
 ):
     ix = lax.axis_index("gx")
@@ -58,18 +114,19 @@
     def at(dx, dy):
         return {"gx": lax.rem(ix + dx + nx, nx), "gy": lax.rem(iy + dy + ny, ny)}
 
-    barrier = pltpu.get_barrier_semaphore()
-    for dx, dy in SIDES:
-        pl.semaphore_signal(
-            barrier, inc=1, device_id=at(dx, dy), device_id_type=pl.DeviceIdType.MESH
-        )
     loads = []
     for n, (src, dst) in enumerate(
         ((cell_h, cell), (frac_h, frac), (force_h, force), (owner_h, owner), (vel_h, vel))
     ):
         loads.append(pltpu.make_async_copy(src, dst, in_sem.at[n]))
         loads[-1].start()
-    for load in loads[:4]:
+    barrier = pltpu.get_barrier_semaphore()
+    for dx, dy in SIDES:
+        pl.semaphore_signal(
+            barrier, inc=1, device_id=at(dx, dy), device_id_type=pl.DeviceIdType.MESH
+        )
+    matrices(w_in, w_out, w_place, w_adv, w_t, w_s, w_fix)
+    for load in loads:
         load.wait()
 
     mine = jnp.where(owner[...] == ix * ny + iy, 1.0, 0.0)
@@ -97,10 +154,10 @@
     strips = ((512, -26.0), (528, -10.0), (640, 122.0), (656, 138.0))
 
     def operands(r, _):
-        lanes = pl.ds(pl.multiple_of(r * LANES, LANES), LANES)
+        lanes = slice(r * LANES, r * LANES + LANES)
 
         def row(n):
-            return jnp.broadcast_to(q32[n, pl.ds(r, 1), :], (16, LANES))
+            return jnp.broadcast_to(q32[n, r : r + 1, :], (16, LANES))
 
         dx0 = rows16 - row(0)
         lw = [[row(10 + 4 * c + k).astype(BF) for k in range(4)] for c in range(2)]
@@ -120,16 +177,16 @@
                 wy_hot[pl.ds(first_row + step * l, 16), lanes] = w * lv[l]
         return 0
 
-    lax.fori_loop(0, 16, operands, 0)
-
-    loads[4].wait()
+    for r in range(16):
+        operands(r, 0)
+
     lane64 = lax.broadcasted_iota(jnp.int32, (64, LANES), 1)
     level64, j64 = lane64 // 32, lane64 % 32
+    both = lax.dot_general(
+        left[...], wy_hot[...], (((1,), (1,)), ((), ())), preferred_element_type=F32
+    )
     for c in range(2):
-        spread = lax.dot_general(
-            left[pl.ds(96 * c, 96), :], wy_hot[...], (((1,), (1,)), ((), ())),
-            preferred_element_type=F32,
-        )
+        spread = both[96 * c : 96 * c + 96]
         mv[c] = spread
         low_part = jnp.zeros((64, LANES), F32)
         high_part = jnp.zeros((64, LANES), F32)
@@ -146,28 +203,15 @@
         mv[c, 16:80, 512:640] = spread[16:80, 512:640] + low_part
         mv[c, 16:80, 640:768] = spread[16:80, 640:768] + high_part
 
-    lane = lax.broadcasted_iota(jnp.int32, (96, LANES), 1)
-    level, j = lane // 32, lane % 32
-    strip0 = [mv[c, :, 512:640] for c in range(2)]
-    strip1 = [mv[c, :, 640:768] for c in range(2)]
-    near = j < 16
-    outer = [
-        jnp.where(near, pltpu.roll(strip1[0], 122, 1), pltpu.roll(strip1[1], 10, 1)),
-        jnp.where(near, pltpu.roll(strip0[0], 118, 1), pltpu.roll(strip0[1], 6, 1)),
-    ]
-    inner = [[], []]
     for c in range(2):
-        up = pltpu.roll(strip1[c], 20, 1)
-        down = pltpu.roll(strip0[c], 108, 1)
-        for l in range(4):
-            t = mv[c, :, 128 * l : 128 * l + 128]
-            up = jnp.where((level == l) & (j < 26), pltpu.roll(t, (32 * l + 26) % LANES, 1), up)
-            down = jnp.where((level == l) & (j >= 6), pltpu.roll(t, 32 * l + 6, 1), down)
-        inner[0].append(up)
-        inner[1].append(down)
+        mvb[96 * c : 96 * c + 96, :] = mv[c].astype(BF)
+    inner = jnp.dot(mvb[...], w_in[...], preferred_element_type=F32)
+    outer = jnp.dot(mvb[0:96, 512:768], w_out[0:256, :], preferred_element_type=F32)
+    outer = outer + jnp.dot(mvb[96:192, 512:768], w_out[256:512, :], preferred_element_type=F32)
     filler = jnp.zeros((8, LANES), F32)
     for side in range(2):
-        parts = [inner[side][0], inner[side][1], outer[side]]
+        ls = slice(128 * side, 128 * side + 128)
+        parts = [inner[0:96, ls], inner[96:192, ls], outer[:, ls]]
         py[side] = jnp.concatenate(parts, axis=0).astype(BF)
         for n in range(4):
             dx, dy = SIDES[4 + n]
@@ -235,77 +279,116 @@
     rxf = [rx[n].astype(F32) for n in range(2)]
     from_y = [[r[96 * p : 96 * p + 96] for p in range(3)] for r in ryf]
     from_c = [[r[40 * p : 40 * p + 40] for p in range(3)] for r in rcf]
-    pack16 = [
+    placed = jnp.dot(
         jnp.concatenate(
-            joined(from_y[side][2], from_c[corner[0, side]][2], from_c[corner[1, side]][2]), axis=0
-        )
-        for side in range(2)
-    ]
-    lane112 = lax.broadcasted_iota(jnp.int32, (112, LANES), 1)
-
-    def rolled(q, by):
-        return pltpu.roll(q, by % LANES, 1) if by % LANES else q
-
-    for c in range(2):
-        for t in range(6):
+            [
+                jnp.concatenate([ry[side, 192:288, :] for side in range(2)], axis=1),
+                jnp.concatenate([rc[corner[0, side], 80:128, :] for side in range(2)], axis=1),
+                jnp.concatenate([rc[corner[1, side], 80:128, :] for side in range(2)], axis=1),
+            ],
+            axis=0,
+        ),
+        w_place[...],
+        preferred_element_type=F32,
+    )
+
+    for t in range(6):
+        for c in range(2):
             ls = slice(128 * t, 128 * t + 128)
             mid = mv[c, :, ls]
             first, last = (r[40 * c : 40 * c + 40, ls] for r in rxf)
             if t < 4:
-                a = jnp.concatenate(joined(mid, first, last), axis=0)
-                g = 32 * t + 16 * c
-                a = a + jnp.where(lane112 < 16, rolled(pack16[0], -g), 0.0)
-                a = a + jnp.where(lane112 >= 112, rolled(pack16[1], 112 - g), 0.0)
+                ps = slice(512 * c + 128 * t, 512 * c + 128 * t + 128)
+                mid = mid + placed[0:96, ps]
+                first = first + placed[96:136, ps]
+                last = last + placed[144:184, ps]
             else:
                 side = t - 4
                 mid = mid + from_y[side][c]
                 first = first + from_c[corner[0, side]][c]
                 last = last + from_c[corner[1, side]][c]
-                a = jnp.concatenate(joined(mid, first, last), axis=0)
+            a = jnp.concatenate(joined(mid, first, last), axis=0)
             mt[c, t, 8:120, :] = a
+            high, low = pieces(a)
+            sp[t, 112 * c : 112 * c + 112, 0:128] = high
+            sp[t, 112 * c : 112 * c + 112, 128:256] = low
 
     for t in range(6):
-        a = COURANT * mt[0, t, 8:120, :]
-        b = COURANT * mt[1, t, 8:120, :]
-        ap, am = jnp.maximum(a, 0.0), jnp.minimum(a, 0.0)
-        bp, bm = jnp.maximum(b, 0.0), jnp.minimum(b, 0.0)
-        for c in range(2):
-            q = mt[c, t, 8:120, :]
-            change = ap * (q - mt[c, t, 7:119, :]) + am * (mt[c, t, 9:121, :] - q)
-            change = change + bp * (q - rolled(q, 1)) + bm * (rolled(q, -1) - q)
-            ca[c, t, 8:120, :] = q - change
-
-    def around(ref, c, t, lo, hi):
-        q = ref[c, t, lo:hi, :]
-        total = ref[c, t, lo - 1 : hi - 1, :] + ref[c, t, lo + 1 : hi + 1, :]
-        total = total + rolled(q, 1) + rolled(q, -1)
+        steps = jnp.dot(sp[t], w_adv[...], preferred_element_type=F32)
+        for lo in range(0, 112, 16):
+            here = slice(lo + 8, lo + 24)
+            a = COURANT * mt[0, t, here, :]
+            b = COURANT * mt[1, t, here, :]
+            ap, am = jnp.maximum(a, 0.0), jnp.minimum(a, 0.0)
+            bp, bm = jnp.maximum(b, 0.0), jnp.minimum(b, 0.0)
+            for c in range(2):
+                q = mt[c, t, here, :]
+                row = 112 * c + lo
+                change = ap * (q - mt[c, t, lo + 7 : lo + 23, :]) + am * (mt[c, t, lo + 9 : lo + 25, :] - q)
+                change = change + bp * steps[row : row + 16, 0:128] + bm * steps[row : row + 16, 128:256]
+                value = q - change
+                ca[c, t, here, :] = value
+                high, low = pieces(value)
+                ws[t, row : row + 16, 0:128] = high
+                ws[t, row : row + 16, 128:256] = low
+
+    scale = 1.0 / (1.0 + 6.0 * VISCOUS)
+
+    def sweep(ref, beside, t, c, lo, row):
+        here = slice(lo + 8, lo + 24)
+        total = ref[c, t, lo + 7 : lo + 23, :] + ref[c, t, lo + 9 : lo + 25, :]
+        total = total + beside[row : row + 16]
         if t < 4:
-            return total + ref[c, min(t + 1, 3), lo:hi, :] + ref[c, max(t - 1, 0), lo:hi, :]
-        lanes = lax.broadcasted_iota(jnp.int32, (hi - lo, LANES), 1)
-        total = total + jnp.where(lanes >= 96, q, rolled(q, -32))
-        return total + jnp.where(lanes < 32, q, rolled(q, 32))
-
-    scale = 1.0 / (1.0 + 6.0 * VISCOUS)
-    for c in range(2):
-        for t in range(6):
-            w1[c, t, 8:120, :] = (ca[c, t, 8:120, :] + VISCOUS * around(ca, c, t, 8, 120)) * scale
-    for c in range(2):
-        done = [
-            (ca[c, t, 16:112, :] + VISCOUS * around(w1, c, t, 16, 112)) * scale for t in (4, 5)
-        ]
-        for l in range(4):
-            w2 = (ca[c, l, 16:112, :] + VISCOUS * around(w1, c, l, 16, 112)) * scale
-            w2 = jnp.where(lane < 3, rolled(done[0], -(32 * l + 26)), w2)
-            w2 = jnp.where(lane >= 125, rolled(done[1], 122 - 32 * l), w2)
-            out_v[l, c] = w2[16:80]
-            ta[c, :, 128 * l : 128 * l + 128] = w2.astype(BF)
-        ta[c, :, 512:640] = jnp.where((j >= 10) & (j < 26), done[0], 0.0).astype(BF)
-        ta[c, :, 640:768] = jnp.where((j >= 6) & (j < 22), done[1], 0.0).astype(BF)
+            total = total + (ref[c, min(t + 1, 3), here, :] + ref[c, max(t - 1, 0), here, :])
+        return scale * ca[c, t, here, :] + (scale * VISCOUS) * total
+
+    for t in range(6):
+        beside = jnp.dot(ws[t], (w_t if t < 4 else w_s)[...], preferred_element_type=F32)
+        for c in range(2):
+            for lo in range(0, 112, 16):
+                value = sweep(ca, beside, t, c, lo, 112 * c + lo)
+                w1[c, t, lo + 8 : lo + 24, :] = value
+                high, low = pieces(value)
+                sp[t, 112 * c + lo : 112 * c + lo + 16, 0:128] = high
+                sp[t, 112 * c + lo : 112 * c + lo + 16, 128:256] = low
+
+    lane16 = lax.broadcasted_iota(jnp.int32, (16, LANES), 1)
+    j16 = lane16 % 32
+    keep = ((j16 >= 10) & (j16 < 26), (j16 >= 6) & (j16 < 22))
+    for t in (4, 5):
+        ls = slice(128 * (t - 4), 128 * (t - 4) + 128)
+        beside = jnp.dot(sp[t], w_s[...], preferred_element_type=F32)
+        for c in range(2):
+            values = [
+                sweep(w1, beside, t, c, lo, 112 * c + lo) for lo in range(0, 112, 16)
+            ]
+            whole = jnp.concatenate(values, axis=0)[8:104]
+            high, low = pieces(whole)
+            ws[0, 96 * c : 96 * c + 96, ls] = high
+            ws[1, 96 * c : 96 * c + 96, ls] = low
+            kept = jnp.where(keep[t - 4], whole.reshape(6, 16, LANES), 0.0).reshape(96, LANES)
+            ta[96 * c : 96 * c + 96, 128 * t : 128 * t + 128] = kept.astype(BF)
+    ends = jnp.dot(ws[0, 0:192, :], w_fix[...], preferred_element_type=F32)
+    ends = ends + jnp.dot(ws[1, 0:192, :], w_fix[...], preferred_element_type=F32)
+    lane = lax.broadcasted_iota(jnp.int32, (96, LANES), 1)
+    inside = (lane >= 3) & (lane < 125)
+    for t in range(4):
+        ls = slice(128 * t, 128 * t + 128)
+        beside = jnp.dot(sp[t], w_t[...], preferred_element_type=F32)
+        for c in range(2):
+            values = [
+                sweep(w1, beside, t, c, lo, 112 * c + lo) for lo in range(0, 112, 16)
+            ]
+            whole = jnp.concatenate(values, axis=0)[8:104]
+            whole = jnp.where(inside, whole, ends[96 * c : 96 * c + 96, ls])
+            out_v[t, c] = whole[16:80]
+            ta[96 * c : 96 * c + 96, ls] = whole.astype(BF)
 
     for r in range(4):
         lanes = slice(512 * r, 512 * r + 512)
-        for c in range(2):
-            part = jnp.dot(ta[c], wy_hot[:, lanes], preferred_element_type=F32)
+        both = jnp.dot(ta[...], wy_hot[:, lanes], preferred_element_type=F32)
+        for c in range(2):
+            part = both[96 * c : 96 * c + 96]
             summed = jnp.sum(part * wx_hot[:, lanes], axis=0, keepdims=True)
             for i in range(4):
                 out_m[c, 4 * r + i : 4 * r + i + 1, :] = summed[:, LANES * i : LANES * i + LANES]
@@ -334,6 +417,7 @@
             pltpu.VMEM((96, 2048), F32),
             pltpu.VMEM((768, 2048), BF),
             pltpu.VMEM((2, 96, 768), F32),
+            pltpu.VMEM((192, 768), BF),
             pltpu.VMEM((2, 80, 768), BF),
             pltpu.VMEM((2, 288, 128), BF),
             pltpu.VMEM((4, 128, 128), BF),
@@ -343,7 +427,16 @@
             pltpu.VMEM((2, 6, 128, 128), F32),
             pltpu.VMEM((2, 6, 128, 128), F32),
             pltpu.VMEM((2, 6, 128, 128), F32),
-            pltpu.VMEM((2, 96, 768), BF),
+            pltpu.VMEM((6, 224, 256), BF),
+            pltpu.VMEM((6, 224, 256), BF),
+            pltpu.VMEM((192, 768), BF),
+            pltpu.VMEM((768, 256), BF),
+            pltpu.VMEM((512, 256), BF),
+            pltpu.VMEM((256, 1024), BF),
+            pltpu.VMEM((256, 256), BF),
+            pltpu.VMEM((256, 128), BF),
+            pltpu.VMEM((256, 128), BF),
+            pltpu.VMEM((256, 512), BF),
             pltpu.SemaphoreType.DMA((5,)),
             pltpu.SemaphoreType.DMA((8,)),
             pltpu.SemaphoreType.DMA((8,)),

time: 23.4 us -> 23.1 us (0.987)
  the two profiles are of different devices: /device:TPU:56 before, /device:TPU:1 now
where the time goes in v4:
time: 23.1 us; the launch traced here: 22.9 us
  Pallas kernels  21 us (91%)
  local copies, waits for them, and re-layouts  1.31 us (6%)
  between operations  0.64 us (3%)
    pallas_call x1, Pallas kernels, body(): pl.pallas_call(functools.partial(kernel, nx, ny), out_shape=(jax.ShapeDty...  21 us
    unnamed x2, local copies, waits for them, and re-layouts  1.31 us

profile of v4, /device:TPU:1, one launch (start us, length us, event | category | flops | bytes accessed | tf_op | source)
XLA Modules:
  0.0 22.9 jit_solution(1988215987736834032)
XLA Ops:
  0.6 21.0 %fish_step.1 = (f32[4,2,64,128]{3,2,1,0:T(8,128)S(1)}, f32[2,16,128]{2,1,0:T(8,128)S(1)}) custom-call(f32[4,2,64,128]{3,2,1,0:T(8,128)} %vel_h.1, s32[3,16,128]{2,1,0:T(8,128)} %bitcast.6, f32[2,16,128]{2,1,0:T(8,128)} %bitcast.7, f32[2,16,128]{2,1,0:T(8,128)} %bitcast.8, s32[6,128]{1,0:T(8,128)} %bitcast.9), custom_call_target="tpu_custom_call" | custom-call | tf_op jit(solution)/shard_map/fish_step/pallas_call | solution.py:401
  21.6 0.7 %copy.10 = f32[4,2,64,128]{3,2,1,0:T(8,128)} copy(f32[4,2,64,128]{3,2,1,0:T(8,128)S(1)} %get-tuple-element.10) | data formatting | bytes 524288
  22.3 0.6 %copy.11 = f32[2,1,1,2048]{3,2,1,0:T(1,128)} copy(f32[2,1,1,2048]{3,2,1,0:T(1,128)S(1)} %bitcast.5) | data formatting | bytes 32768

commit v5 on v4

--- a/solution.py
+++ b/solution.py
@@ -17,6 +17,7 @@
 F32 = jnp.float32
 
 SIDES = [(1, 0), (-1, 0), (0, 1), (0, -1), (1, 1), (-1, 1), (1, -1), (-1, -1)]
+UPPER = [(1, 0), (1, 1), (1, -1), (0, 1)]
 
 
 def half_angle(t):
@@ -106,7 +107,7 @@
     vel, cell, frac, force, owner,
     q32, left, wx_hot, wy_hot, mv, mvb, px, py, pc, rx, ry, rc,
     mt, ca, w1, sp, ws, ta, w_in, w_out, w_place, w_adv, w_t, w_s, w_fix,
-    in_sem, send1, recv1,
+    in_sem, send1, recv1, here_sem,
 ):
     ix = lax.axis_index("gx")
     iy = lax.axis_index("gy")
@@ -121,9 +122,9 @@
         loads.append(pltpu.make_async_copy(src, dst, in_sem.at[n]))
         loads[-1].start()
     barrier = pltpu.get_barrier_semaphore()
-    for dx, dy in SIDES:
+    for dx, dy in UPPER:
         pl.semaphore_signal(
-            barrier, inc=1, device_id=at(dx, dy), device_id_type=pl.DeviceIdType.MESH
+            barrier, inc=1, device_id=at(-dx, -dy), device_id_type=pl.DeviceIdType.MESH
         )
     matrices(w_in, w_out, w_place, w_adv, w_t, w_s, w_fix)
     for load in loads:
@@ -221,7 +222,11 @@
     for n, lo in enumerate((56, 0)):
         px[n] = jnp.concatenate([mv[0, lo : lo + 40, :], mv[1, lo : lo + 40, :]], axis=0).astype(BF)
 
-    pl.semaphore_wait(barrier, 8)
+    pl.semaphore_wait(barrier, 4)
+    for n, (dx, dy) in enumerate(UPPER):
+        pl.semaphore_signal(
+            here_sem.at[n], inc=1, device_id=at(dx, dy), device_id_type=pl.DeviceIdType.MESH
+        )
 
     copies = []
 
@@ -233,12 +238,17 @@
         copy.start()
         copies.append(copy)
 
-    for n in range(4):
-        send(4 + n, pc.at[n], rc.at[n], *SIDES[4 + n])
-    for n in range(2):
-        send(2 + n, py.at[n], ry.at[n], *SIDES[2 + n])
-    for n in range(2):
-        send(n, px.at[n], rx.at[n], *SIDES[n])
+    def send_to(dx, dy):
+        n = SIDES.index((dx, dy))
+        if n < 2:
+            send(n, px.at[n], rx.at[n], dx, dy)
+        elif n < 4:
+            send(n, py.at[n - 2], ry.at[n - 2], dx, dy)
+        else:
+            send(n, pc.at[n - 4], rc.at[n - 4], dx, dy)
+
+    for dx, dy in UPPER:
+        send_to(dx, dy)
 
     rows8 = lax.broadcasted_iota(jnp.int32, (8, LANES), 0).astype(F32)
 
@@ -260,6 +270,10 @@
             for t in range(6):
                 ref[c, t, 0:8, :] = jnp.zeros((8, LANES), F32)
                 ref[c, t, 120:128, :] = jnp.zeros((8, LANES), F32)
+
+    for n, (dx, dy) in enumerate(UPPER):
+        pl.semaphore_wait(here_sem.at[n], 1)
+        send_to(-dx, -dy)
 
     for copy in copies:
         copy.wait()
@@ -440,6 +454,7 @@
             pltpu.SemaphoreType.DMA((5,)),
             pltpu.SemaphoreType.DMA((8,)),
             pltpu.SemaphoreType.DMA((8,)),
+            pltpu.SemaphoreType.REGULAR((4,)),
         ],
         compiler_params=pltpu.CompilerParams(
             collective_id=0, has_side_effects=True, vmem_limit_bytes=32 * 1024 * 1024

time: 23.1 us -> 24.7 us (1.069)
  the two profiles are of different devices: /device:TPU:1 before, /device:TPU:28 now
where the time goes in v5:
time: 24.7 us; the launch traced here: 24.6 us
  Pallas kernels  22.6 us (91%)
  local copies, waits for them, and re-layouts  1.31 us (5%)
  between operations  0.64 us (3%)
    pallas_call x1, Pallas kernels, body(): pl.pallas_call(functools.partial(kernel, nx, ny), out_shape=(jax.ShapeDty...  22.6 us
    unnamed x2, local copies, waits for them, and re-layouts  1.31 us

profile of v5, /device:TPU:28, one launch (start us, length us, event | category | flops | bytes accessed | tf_op | source)
XLA Modules:
  0.0 24.6 jit_solution(1696277090982891328)
XLA Ops:
  0.6 22.6 %fish_step.1 = (f32[4,2,64,128]{3,2,1,0:T(8,128)S(1)}, f32[2,16,128]{2,1,0:T(8,128)S(1)}) custom-call(f32[4,2,64,128]{3,2,1,0:T(8,128)} %vel_h.1, s32[3,16,128]{2,1,0:T(8,128)} %bitcast.6, f32[2,16,128]{2,1,0:T(8,128)} %bitcast.7, f32[2,16,128]{2,1,0:T(8,128)} %bitcast.8, s32[6,128]{1,0:T(8,128)} %bitcast.9), custom_call_target="tpu_custom_call" | custom-call | tf_op jit(solution)/shard_map/fish_step/pallas_call | solution.py:415
  23.2 0.7 %copy.10 = f32[4,2,64,128]{3,2,1,0:T(8,128)} copy(f32[4,2,64,128]{3,2,1,0:T(8,128)S(1)} %get-tuple-element.10) | data formatting | bytes 524288
  23.9 0.6 %copy.11 = f32[2,1,1,2048]{3,2,1,0:T(1,128)} copy(f32[2,1,1,2048]{3,2,1,0:T(1,128)S(1)} %bitcast.5) | data formatting | bytes 32768

commit v6 on v5

--- a/solution.py
+++ b/solution.py
@@ -17,7 +17,7 @@
 F32 = jnp.float32
 
 SIDES = [(1, 0), (-1, 0), (0, 1), (0, -1), (1, 1), (-1, 1), (1, -1), (-1, -1)]
-UPPER = [(1, 0), (1, 1), (1, -1), (0, 1)]
+UPPER = [(0, 1), (1, 0), (1, 1), (1, -1)]
 
 
 def half_angle(t):
@@ -103,10 +103,10 @@
 def kernel(
     nx, ny,
     vel_h, cell_h, frac_h, force_h, owner_h,
-    out_v, out_m,
+    out_v, ta, wy_hot, wx_hot,
     vel, cell, frac, force, owner,
-    q32, left, wx_hot, wy_hot, mv, mvb, px, py, pc, rx, ry, rc,
-    mt, ca, w1, sp, ws, ta, w_in, w_out, w_place, w_adv, w_t, w_s, w_fix,
+    q32, left, mv, mvb, px, py, pc, rx, ry, rc,
+    mt, ca, w1, sp, ws, ends_in, w_in, w_out, w_place, w_adv, w_t, w_s, w_fix,
     in_sem, send1, recv1, here_sem,
 ):
     ix = lax.axis_index("gx")
@@ -247,8 +247,12 @@
         else:
             send(n, pc.at[n - 4], rc.at[n - 4], dx, dy)
 
-    for dx, dy in UPPER:
+    for dx, dy in UPPER[1:] + UPPER[:1]:
         send_to(dx, dy)
+
+    for n, (dx, dy) in enumerate(UPPER):
+        pl.semaphore_wait(here_sem.at[n], 1)
+        send_to(-dx, -dy)
 
     rows8 = lax.broadcasted_iota(jnp.int32, (8, LANES), 0).astype(F32)
 
@@ -270,10 +274,6 @@
             for t in range(6):
                 ref[c, t, 0:8, :] = jnp.zeros((8, LANES), F32)
                 ref[c, t, 120:128, :] = jnp.zeros((8, LANES), F32)
-
-    for n, (dx, dy) in enumerate(UPPER):
-        pl.semaphore_wait(here_sem.at[n], 1)
-        send_to(-dx, -dy)
 
     for copy in copies:
         copy.wait()
@@ -306,7 +306,7 @@
         preferred_element_type=F32,
     )
 
-    for t in range(6):
+    def assemble(t):
         for c in range(2):
             ls = slice(128 * t, 128 * t + 128)
             mid = mv[c, :, ls]
@@ -327,20 +327,23 @@
             sp[t, 112 * c : 112 * c + 112, 0:128] = high
             sp[t, 112 * c : 112 * c + 112, 128:256] = low
 
-    for t in range(6):
+    def advect(t):
         steps = jnp.dot(sp[t], w_adv[...], preferred_element_type=F32)
         for lo in range(0, 112, 16):
             here = slice(lo + 8, lo + 24)
             a = COURANT * mt[0, t, here, :]
             b = COURANT * mt[1, t, here, :]
-            ap, am = jnp.maximum(a, 0.0), jnp.minimum(a, 0.0)
-            bp, bm = jnp.maximum(b, 0.0), jnp.minimum(b, 0.0)
+            forth, right = a > 0.0, b > 0.0
             for c in range(2):
                 q = mt[c, t, here, :]
                 row = 112 * c + lo
-                change = ap * (q - mt[c, t, lo + 7 : lo + 23, :]) + am * (mt[c, t, lo + 9 : lo + 25, :] - q)
-                change = change + bp * steps[row : row + 16, 0:128] + bm * steps[row : row + 16, 128:256]
-                value = q - change
+                step_x = jnp.where(
+                    forth, q - mt[c, t, lo + 7 : lo + 23, :], mt[c, t, lo + 9 : lo + 25, :] - q
+                )
+                step_y = jnp.where(
+                    right, steps[row : row + 16, 0:128], steps[row : row + 16, 128:256]
+                )
+                value = q - (a * step_x + b * step_y)
                 ca[c, t, here, :] = value
                 high, low = pieces(value)
                 ws[t, row : row + 16, 0:128] = high
@@ -356,7 +359,7 @@
             total = total + (ref[c, min(t + 1, 3), here, :] + ref[c, max(t - 1, 0), here, :])
         return scale * ca[c, t, here, :] + (scale * VISCOUS) * total
 
-    for t in range(6):
+    def first_sweep(t):
         beside = jnp.dot(ws[t], (w_t if t < 4 else w_s)[...], preferred_element_type=F32)
         for c in range(2):
             for lo in range(0, 112, 16):
@@ -366,38 +369,53 @@
                 sp[t, 112 * c + lo : 112 * c + lo + 16, 0:128] = high
                 sp[t, 112 * c + lo : 112 * c + lo + 16, 128:256] = low
 
+    def second_sweep(t, c, beside):
+        values = [sweep(w1, beside, t, c, lo, 112 * c + lo) for lo in range(0, 112, 16)]
+        return jnp.concatenate(values, axis=0)[8:104]
+
     lane16 = lax.broadcasted_iota(jnp.int32, (16, LANES), 1)
     j16 = lane16 % 32
     keep = ((j16 >= 10) & (j16 < 26), (j16 >= 6) & (j16 < 22))
+    assemble(4)
+    assemble(5)
+    advect(4)
+    advect(5)
+    assemble(0)
+    first_sweep(4)
+    first_sweep(5)
+    for t in (1, 2, 3):
+        assemble(t)
     for t in (4, 5):
         ls = slice(128 * (t - 4), 128 * (t - 4) + 128)
         beside = jnp.dot(sp[t], w_s[...], preferred_element_type=F32)
         for c in range(2):
-            values = [
-                sweep(w1, beside, t, c, lo, 112 * c + lo) for lo in range(0, 112, 16)
-            ]
-            whole = jnp.concatenate(values, axis=0)[8:104]
+            whole = second_sweep(t, c, beside)
             high, low = pieces(whole)
-            ws[0, 96 * c : 96 * c + 96, ls] = high
-            ws[1, 96 * c : 96 * c + 96, ls] = low
+            ends_in[0, 96 * c : 96 * c + 96, ls] = high
+            ends_in[1, 96 * c : 96 * c + 96, ls] = low
             kept = jnp.where(keep[t - 4], whole.reshape(6, 16, LANES), 0.0).reshape(96, LANES)
             ta[96 * c : 96 * c + 96, 128 * t : 128 * t + 128] = kept.astype(BF)
-    ends = jnp.dot(ws[0, 0:192, :], w_fix[...], preferred_element_type=F32)
-    ends = ends + jnp.dot(ws[1, 0:192, :], w_fix[...], preferred_element_type=F32)
+    for t in range(4):
+        advect(t)
+    ends = jnp.dot(ends_in[0], w_fix[...], preferred_element_type=F32)
+    ends = ends + jnp.dot(ends_in[1], w_fix[...], preferred_element_type=F32)
+    for t in range(4):
+        first_sweep(t)
     lane = lax.broadcasted_iota(jnp.int32, (96, LANES), 1)
     inside = (lane >= 3) & (lane < 125)
     for t in range(4):
         ls = slice(128 * t, 128 * t + 128)
         beside = jnp.dot(sp[t], w_t[...], preferred_element_type=F32)
         for c in range(2):
-            values = [
-                sweep(w1, beside, t, c, lo, 112 * c + lo) for lo in range(0, 112, 16)
-            ]
-            whole = jnp.concatenate(values, axis=0)[8:104]
+            whole = second_sweep(t, c, beside)
             whole = jnp.where(inside, whole, ends[96 * c : 96 * c + 96, ls])
             out_v[t, c] = whole[16:80]
             ta[96 * c : 96 * c + 96, ls] = whole.astype(BF)
 
+
+def sampling(v, ta, wy_hot, wx_hot, out_v, out_m, out_sem):
+    copy = pltpu.make_async_copy(v, out_v, out_sem)
+    copy.start()
     for r in range(4):
         lanes = slice(512 * r, 512 * r + 512)
         both = jnp.dot(ta[...], wy_hot[:, lanes], preferred_element_type=F32)
@@ -406,20 +424,23 @@
             summed = jnp.sum(part * wx_hot[:, lanes], axis=0, keepdims=True)
             for i in range(4):
                 out_m[c, 4 * r + i : 4 * r + i + 1, :] = summed[:, LANES * i : LANES * i + LANES]
+    copy.wait()
 
 
 def body(velocity, marker_cell, marker_frac, marker_force, fish_owner):
     nx = lax.axis_size("gx")
     ny = lax.axis_size("gy")
     vm = pl.BlockSpec(memory_space=pltpu.VMEM)
-    out_v, out_m = pl.pallas_call(
+    v, ta, wy_hot, wx_hot = pl.pallas_call(
         functools.partial(kernel, nx, ny),
         out_shape=(
             jax.ShapeDtypeStruct((4, 2, 64, 128), F32),
-            jax.ShapeDtypeStruct((2, 16, 128), F32),
+            jax.ShapeDtypeStruct((192, 768), BF),
+            jax.ShapeDtypeStruct((768, 2048), BF),
+            jax.ShapeDtypeStruct((96, 2048), F32),
         ),
         in_specs=[pl.BlockSpec(memory_space=pltpu.HBM)] * 5,
-        out_specs=(vm, vm),
+        out_specs=(vm, vm, vm, vm),
         scratch_shapes=[
             pltpu.VMEM((4, 2, 64, 128), F32),
             pltpu.VMEM((3, 16, 128), jnp.int32),
@@ -428,8 +449,6 @@
             pltpu.VMEM((6, 128), jnp.int32),
             pltpu.VMEM((23, 16, 128), F32),
             pltpu.VMEM((192, 2048), BF),
-            pltpu.VMEM((96, 2048), F32),
-            pltpu.VMEM((768, 2048), BF),
             pltpu.VMEM((2, 96, 768), F32),
             pltpu.VMEM((192, 768), BF),
             pltpu.VMEM((2, 80, 768), BF),
@@ -443,7 +462,7 @@
             pltpu.VMEM((2, 6, 128, 128), F32),
             pltpu.VMEM((6, 224, 256), BF),
             pltpu.VMEM((6, 224, 256), BF),
-            pltpu.VMEM((192, 768), BF),
+            pltpu.VMEM((2, 192, 256), BF),
             pltpu.VMEM((768, 256), BF),
             pltpu.VMEM((512, 256), BF),
             pltpu.VMEM((256, 1024), BF),
@@ -457,7 +476,7 @@
             pltpu.SemaphoreType.REGULAR((4,)),
         ],
         compiler_params=pltpu.CompilerParams(
-            collective_id=0, has_side_effects=True, vmem_limit_bytes=32 * 1024 * 1024
+            collective_id=0, has_side_effects=True, vmem_limit_bytes=24 * 1024 * 1024
         ),
         name="fish_step",
     )(
@@ -467,6 +486,18 @@
         pltpu.with_memory_space_constraint(marker_force.reshape(2, 16, 128), pltpu.HBM),
         pltpu.with_memory_space_constraint(fish_owner.reshape(6, 128), pltpu.HBM),
     )
+    out_v, out_m = pl.pallas_call(
+        sampling,
+        out_shape=(
+            jax.ShapeDtypeStruct((4, 2, 64, 128), F32),
+            jax.ShapeDtypeStruct((2, 16, 128), F32),
+        ),
+        in_specs=[vm] * 4,
+        out_specs=(pl.BlockSpec(memory_space=pltpu.HBM), vm),
+        scratch_shapes=[pltpu.SemaphoreType.DMA],
+        compiler_params=pltpu.CompilerParams(vmem_limit_bytes=8 * 1024 * 1024),
+        name="fish_sample",
+    )(v, ta, wy_hot, wx_hot)
     return out_v, out_m.reshape(2, 1, 1, 2048)
 
 

time: 24.7 us -> 22.2 us (0.90)
  the two profiles are of different devices: /device:TPU:28 before, /device:TPU:56 now
where the time goes in v6:
time: 22.2 us; the launch traced here: 22.1 us
  Pallas kernels  21.4 us (96%)
  between operations  0.64 us (3%)
    pallas_call x1, Pallas kernels, body(): pl.pallas_call(functools.partial(kernel, nx, ny), out_shape=(jax.ShapeDty...  19.5 us
    pallas_call x1, Pallas kernels, body(): pl.pallas_call(sampling, out_shape=(jax.ShapeDtypeStruct((4, 2, 64, 128),...  1.92 us

profile of v6, /device:TPU:56, one launch (start us, length us, event | category | flops | bytes accessed | tf_op | source)
XLA Modules:
  0.0 22.1 jit_solution(13925252227516499736)
XLA Ops:
  0.6 19.5 %fish_step.1 = (f32[4,2,64,128]{3,2,1,0:T(8,128)S(1)}, bf16[192,768]{1,0:T(8,128)(2,1)S(1)}, bf16[768,2048]{1,0:T(8,128)(2,1)S(1)}, f32[96,2048]{1,0:T(8,128)S(1)}) custom-call(f32[4,2,64,128]{3,2,1,0:T(8,128)} %vel_h.1, s32[3,16,128]{2,1,0:T(8,128)} %bitcast.5, f32[2,16,128]{2,1,0:T(8,128)} %bitcast.6, f32[2,16,128]{2,1,0:T(8,128)} %bitcast.7, s32[6,128]{1,0:T(8,128)} %bitcast.8), custom_call_target="tpu_custom_call" | custom-call | tf_op jit(solution)/shard_map/fish_step/pallas_call | solution.py:434
  20.2 1.9 %fish_sample.1 = (f32[4,2,64,128]{3,2,1,0:T(8,128)}, f32[2,16,128]{2,1,0:T(8,128)}) custom-call(f32[4,2,64,128]{3,2,1,0:T(8,128)S(1)} %get-tuple-element.8.v, bf16[192,768]{1,0:T(8,128)(2,1)S(1)} %get-tuple-element.9.ta, bf16[768,2048]{1,0:T(8,128)(2,1)S(1)} %get-tuple-element.10.wy_hot, f32[96,2048]{1,0:T(8,128)S(1)} %get-tuple-element.11.wx_hot), custom_call_target="tpu_custom_call" | custom-call | tf_op jit(solution)/shard_map/fish_sample/pallas_call | solution.py:489

commit v7 on v6

--- a/solution.py
+++ b/solution.py
@@ -17,7 +17,7 @@
 F32 = jnp.float32
 
 SIDES = [(1, 0), (-1, 0), (0, 1), (0, -1), (1, 1), (-1, 1), (1, -1), (-1, -1)]
-UPPER = [(0, 1), (1, 0), (1, 1), (1, -1)]
+UPPER = [(0, 1), (1, 1), (1, -1), (1, 0)]
 
 
 def half_angle(t):
@@ -228,24 +228,21 @@
             here_sem.at[n], inc=1, device_id=at(dx, dy), device_id_type=pl.DeviceIdType.MESH
         )
 
-    copies = []
-
-    def send(n, src, dst, dx, dy):
+    def send(src, dst, dx, dy):
         copy = pltpu.make_async_remote_copy(
-            src_ref=src, dst_ref=dst, send_sem=send1.at[n], recv_sem=recv1.at[n],
+            src_ref=src, dst_ref=dst, send_sem=send1, recv_sem=recv1,
             device_id=at(dx, dy), device_id_type=pl.DeviceIdType.MESH,
         )
         copy.start()
-        copies.append(copy)
 
     def send_to(dx, dy):
         n = SIDES.index((dx, dy))
         if n < 2:
-            send(n, px.at[n], rx.at[n], dx, dy)
+            send(px.at[n], rx.at[n], dx, dy)
         elif n < 4:
-            send(n, py.at[n - 2], ry.at[n - 2], dx, dy)
+            send(py.at[n - 2], ry.at[n - 2], dx, dy)
         else:
-            send(n, pc.at[n - 4], rc.at[n - 4], dx, dy)
+            send(pc.at[n - 4], rc.at[n - 4], dx, dy)
 
     for dx, dy in UPPER[1:] + UPPER[:1]:
         send_to(dx, dy)
@@ -275,8 +272,9 @@
                 ref[c, t, 0:8, :] = jnp.zeros((8, LANES), F32)
                 ref[c, t, 120:128, :] = jnp.zeros((8, LANES), F32)
 
-    for copy in copies:
-        copy.wait()
+    everything = wy_hot.at[pl.ds(0, 128)]
+    pltpu.make_async_copy(everything, everything, recv1).wait()
+    pltpu.make_async_copy(everything, everything, send1).wait()
 
     corner = {}
     for n in range(4):
@@ -471,8 +469,8 @@
             pltpu.VMEM((256, 128), BF),
             pltpu.VMEM((256, 512), BF),
             pltpu.SemaphoreType.DMA((5,)),
-            pltpu.SemaphoreType.DMA((8,)),
-            pltpu.SemaphoreType.DMA((8,)),
+            pltpu.SemaphoreType.DMA,
+            pltpu.SemaphoreType.DMA,
             pltpu.SemaphoreType.REGULAR((4,)),
         ],
         compiler_params=pltpu.CompilerParams(

time: 22.2 us -> 22.7 us (1.023)
  Pallas kernels: 21.4 us -> 21.9 us
    pallas_call x1, Pallas kernels: 19.5 us -> 20 us  [body(): pl.pallas_call(functools.partial(kernel, nx, ny), out_shape=(jax.ShapeDty...]
where the time goes in v7:
time: 22.7 us; the launch traced here: 22.6 us
  Pallas kernels  21.9 us (96%)
  between operations  0.64 us (3%)
    pallas_call x1, Pallas kernels, body(): pl.pallas_call(functools.partial(kernel, nx, ny), out_shape=(jax.ShapeDty...  20 us
    pallas_call x1, Pallas kernels, body(): pl.pallas_call(sampling, out_shape=(jax.ShapeDtypeStruct((4, 2, 64, 128),...  1.92 us

profile of v7, /device:TPU:56, one launch (start us, length us, event | category | flops | bytes accessed | tf_op | source)
XLA Modules:
  0.0 22.6 jit_solution(15194451568382211867)
XLA Ops:
  0.6 20.0 %fish_step.1 = (f32[4,2,64,128]{3,2,1,0:T(8,128)S(1)}, bf16[192,768]{1,0:T(8,128)(2,1)S(1)}, bf16[768,2048]{1,0:T(8,128)(2,1)S(1)}, f32[96,2048]{1,0:T(8,128)S(1)}) custom-call(f32[4,2,64,128]{3,2,1,0:T(8,128)} %vel_h.1, s32[3,16,128]{2,1,0:T(8,128)} %bitcast.5, f32[2,16,128]{2,1,0:T(8,128)} %bitcast.6, f32[2,16,128]{2,1,0:T(8,128)} %bitcast.7, s32[6,128]{1,0:T(8,128)} %bitcast.8), custom_call_target="tpu_custom_call" | custom-call | tf_op jit(solution)/shard_map/fish_step/pallas_call | solution.py:432
  20.7 1.9 %fish_sample.1 = (f32[4,2,64,128]{3,2,1,0:T(8,128)}, f32[2,16,128]{2,1,0:T(8,128)}) custom-call(f32[4,2,64,128]{3,2,1,0:T(8,128)S(1)} %get-tuple-element.8.v, bf16[192,768]{1,0:T(8,128)(2,1)S(1)} %get-tuple-element.9.ta, bf16[768,2048]{1,0:T(8,128)(2,1)S(1)} %get-tuple-element.10.wy_hot, f32[96,2048]{1,0:T(8,128)S(1)} %get-tuple-element.11.wx_hot), custom_call_target="tpu_custom_call" | custom-call | tf_op jit(solution)/shard_map/fish_sample/pallas_call | solution.py:487

commit v8 on v7

--- a/solution.py
+++ b/solution.py
@@ -17,7 +17,7 @@
 F32 = jnp.float32
 
 SIDES = [(1, 0), (-1, 0), (0, 1), (0, -1), (1, 1), (-1, 1), (1, -1), (-1, -1)]
-UPPER = [(0, 1), (1, 1), (1, -1), (1, 0)]
+UPPER = [(0, 1), (1, 0), (1, 1), (1, -1)]
 
 
 def half_angle(t):
@@ -244,7 +244,7 @@
         else:
             send(pc.at[n - 4], rc.at[n - 4], dx, dy)
 
-    for dx, dy in UPPER[1:] + UPPER[:1]:
+    for dx, dy in UPPER[2:] + UPPER[:2][::-1]:
         send_to(dx, dy)
 
     for n, (dx, dy) in enumerate(UPPER):

time: 22.7 us -> 21.3 us (0.938)
  Pallas kernels: 21.9 us -> 20.5 us
    pallas_call x1, Pallas kernels: 20 us -> 18.6 us  [body(): pl.pallas_call(functools.partial(kernel, nx, ny), out_shape=(jax.ShapeDty...]
where the time goes in v8:
time: 21.3 us; the launch traced here: 21.2 us
  Pallas kernels  20.5 us (96%)
  between operations  0.64 us (3%)
    pallas_call x1, Pallas kernels, body(): pl.pallas_call(functools.partial(kernel, nx, ny), out_shape=(jax.ShapeDty...  18.6 us
    pallas_call x1, Pallas kernels, body(): pl.pallas_call(sampling, out_shape=(jax.ShapeDtypeStruct((4, 2, 64, 128),...  1.92 us

profile of v8, /device:TPU:56, one launch (start us, length us, event | category | flops | bytes accessed | tf_op | source)
XLA Modules:
  0.0 21.2 jit_solution(691342749806756208)
XLA Ops:
  0.6 18.6 %fish_step.1 = (f32[4,2,64,128]{3,2,1,0:T(8,128)S(1)}, bf16[192,768]{1,0:T(8,128)(2,1)S(1)}, bf16[768,2048]{1,0:T(8,128)(2,1)S(1)}, f32[96,2048]{1,0:T(8,128)S(1)}) custom-call(f32[4,2,64,128]{3,2,1,0:T(8,128)} %vel_h.1, s32[3,16,128]{2,1,0:T(8,128)} %bitcast.5, f32[2,16,128]{2,1,0:T(8,128)} %bitcast.6, f32[2,16,128]{2,1,0:T(8,128)} %bitcast.7, s32[6,128]{1,0:T(8,128)} %bitcast.8), custom_call_target="tpu_custom_call" | custom-call | tf_op jit(solution)/shard_map/fish_step/pallas_call | solution.py:432
  19.2 1.9 %fish_sample.1 = (f32[4,2,64,128]{3,2,1,0:T(8,128)}, f32[2,16,128]{2,1,0:T(8,128)}) custom-call(f32[4,2,64,128]{3,2,1,0:T(8,128)S(1)} %get-tuple-element.8.v, bf16[192,768]{1,0:T(8,128)(2,1)S(1)} %get-tuple-element.9.ta, bf16[768,2048]{1,0:T(8,128)(2,1)S(1)} %get-tuple-element.10.wy_hot, f32[96,2048]{1,0:T(8,128)S(1)} %get-tuple-element.11.wx_hot), custom_call_target="tpu_custom_call" | custom-call | tf_op jit(solution)/shard_map/fish_sample/pallas_call | solution.py:487

commit v9 on v8

--- a/solution.py
+++ b/solution.py
@@ -52,16 +52,16 @@
         ref[lo : lo + 16, :] = jnp.where(below == lo, 1.0, 0.0).astype(BF)
 
 
-def matrices(w_in, w_out, w_place, w_adv, w_t, w_s, w_fix):
+def matrices(w_in, w_out, w_place, w_adv, w_t, w_s, w_fix, w_strip, w_edge, w_cut):
     def inner_of(n):
         p, l = n % 32, (n // 32) % 4
-        up = jnp.where(p < 26, 128 * l + p + 102, 640 + 32 * l + p - 20)
-        down = jnp.where(p < 6, 512 + 32 * l + p + 20, 128 * l + p - 6)
+        up = jnp.where(p < 26, 128 * l + p + 102, -1)
+        down = jnp.where(p < 6, -1, 128 * l + p - 6)
         return jnp.where(n < 128, up, down)
 
     def outer_of(n):
         i, c, l = n % 16, (n // 16) % 2, (n // 32) % 4
-        return 256 * c + 32 * l + i + jnp.where(n < 128, 128 + 6, 10)
+        return 128 * c + 16 * l + i + jnp.where(n < 128, 64, 0)
 
     def place_of(n):
         y, l, c = n % 128, (n // 128) % 4, n // 512
@@ -74,6 +74,27 @@
             y < 3, 32 * l + 26 + y, jnp.where(y >= 125, 128 + 32 * l + y - 122, -1)
         )
 
+    def strip_of(n):
+        j, l, side = n % 32, (n // 32) % 4, n // 128
+        i = j - jnp.where(side == 0, 10, 6)
+        return jnp.where((i >= 0) & (i < 16), 64 * side + 16 * l + i, -1)
+
+    def edge_of(n):
+        j, l = n % 32, (n // 32) % 4
+        low = jnp.where(j >= 26, 256 * l + j - 26, -1)
+        return jnp.where(n < 128, low, jnp.where(j < 6, 256 * l + j + 122, -1))
+
+    def cut_of(n):
+        i, l, side = n % 16, (n // 16) % 4, n // 64
+        return 128 * side + 32 * l + i + jnp.where(side == 0, 10, 6)
+
+    for half in range(2):
+        pick(w_strip.at[pl.ds(128 * half, 128)], strip_of)
+    for l in range(4):
+        for half in range(2):
+            rows = pl.ds(256 * l + 128 * half, 128)
+            pick(w_edge.at[rows], lambda n: jnp.where(edge_of(n) // 256 == l, edge_of(n) - 256 * l, -1))
+    pick(w_cut, cut_of)
     pick(w_in, inner_of)
     pick(w_out, outer_of)
     pick(w_place, place_of)
@@ -106,7 +127,8 @@
     out_v, ta, wy_hot, wx_hot,
     vel, cell, frac, force, owner,
     q32, left, mv, mvb, px, py, pc, rx, ry, rc,
-    mt, ca, w1, sp, ws, ends_in, w_in, w_out, w_place, w_adv, w_t, w_s, w_fix,
+    mt, ca, w1, sp, ws, ends_in, beyond, w_in, w_out, w_place, w_adv, w_t, w_s, w_fix,
+    w_strip, w_edge, w_cut,
     in_sem, send1, recv1, here_sem,
 ):
     ix = lax.axis_index("gx")
@@ -126,7 +148,7 @@
         pl.semaphore_signal(
             barrier, inc=1, device_id=at(-dx, -dy), device_id_type=pl.DeviceIdType.MESH
         )
-    matrices(w_in, w_out, w_place, w_adv, w_t, w_s, w_fix)
+    matrices(w_in, w_out, w_place, w_adv, w_t, w_s, w_fix, w_strip, w_edge, w_cut)
     for load in loads:
         load.wait()
 
@@ -152,7 +174,7 @@
 
     rows16 = lax.broadcasted_iota(jnp.int32, (16, LANES), 0).astype(F32)
     zero16 = jnp.zeros((16, LANES), BF)
-    strips = ((512, -26.0), (528, -10.0), (640, 122.0), (656, 138.0))
+    strips = ((512, -16.0), (576, 128.0))
 
     def operands(r, _):
         lanes = slice(r * LANES, r * LANES + LANES)
@@ -160,19 +182,19 @@
         def row(n):
             return jnp.broadcast_to(q32[n, r : r + 1, :], (16, LANES))
 
-        dx0 = rows16 - row(0)
+        dx0 = (rows16 - row(0)).astype(BF)
         lw = [[row(10 + 4 * c + k).astype(BF) for k in range(4)] for c in range(2)]
         for b in range(6):
-            d = (dx0 + 16.0 * b).astype(BF)
+            d = dx0 + jnp.asarray(16.0 * b, BF)
             for c in range(2):
                 left[pl.ds(96 * c + 16 * b, 16), lanes] = chain(d, lw[c], zero16)
-        dy0 = rows16 - row(1)
+        dy0 = (rows16 - row(1)).astype(BF)
         yw = [row(6 + k).astype(BF) for k in range(4)]
         lv = [row(18 + k).astype(BF) for k in range(4)]
-        for b in range(12):
-            base, step = (16.0 * b, 128) if b < 8 else (strips[b - 8][1], 32)
+        for b in range(10):
+            base, step = (16.0 * b, 128) if b < 8 else (strips[b - 8][1], 16)
             first_row = 16 * b if b < 8 else strips[b - 8][0]
-            d = (dy0 + base).astype(BF)
+            d = dy0 + jnp.asarray(base, BF)
             w = chain(d, yw, zero16)
             for l in range(4):
                 wy_hot[pl.ds(first_row + step * l, 16), lanes] = w * lv[l]
@@ -181,34 +203,25 @@
     for r in range(16):
         operands(r, 0)
 
-    lane64 = lax.broadcasted_iota(jnp.int32, (64, LANES), 1)
-    level64, j64 = lane64 // 32, lane64 % 32
     both = lax.dot_general(
         left[...], wy_hot[...], (((1,), (1,)), ((), ())), preferred_element_type=F32
     )
     for c in range(2):
         spread = both[96 * c : 96 * c + 96]
         mv[c] = spread
-        low_part = jnp.zeros((64, LANES), F32)
-        high_part = jnp.zeros((64, LANES), F32)
         for l in range(4):
             ls = slice(128 * l, 128 * l + 128)
             v = vel[l, c]
             mv[c, 16:80, ls] = spread[16:80, ls] + v
-            low_part = jnp.where(
-                (level64 == l) & (j64 >= 26), pltpu.roll(v, 32 * l + 26, 1), low_part
-            )
-            high_part = jnp.where(
-                (level64 == l) & (j64 < 6), pltpu.roll(v, 32 * l + 6, 1), high_part
-            )
-        mv[c, 16:80, 512:640] = spread[16:80, 512:640] + low_part
-        mv[c, 16:80, 640:768] = spread[16:80, 640:768] + high_part
 
     for c in range(2):
         mvb[96 * c : 96 * c + 96, :] = mv[c].astype(BF)
-    inner = jnp.dot(mvb[...], w_in[...], preferred_element_type=F32)
-    outer = jnp.dot(mvb[0:96, 512:768], w_out[0:256, :], preferred_element_type=F32)
-    outer = outer + jnp.dot(mvb[96:192, 512:768], w_out[256:512, :], preferred_element_type=F32)
+    inner = jnp.dot(mvb[:, 0:512], w_in[...], preferred_element_type=F32)
+    outer = jnp.dot(
+        jnp.concatenate([mvb[0:96, 512:640], mvb[96:192, 512:640]], axis=1),
+        w_out[...],
+        preferred_element_type=F32,
+    )
     filler = jnp.zeros((8, LANES), F32)
     for side in range(2):
         ls = slice(128 * side, 128 * side + 128)
@@ -272,7 +285,7 @@
                 ref[c, t, 0:8, :] = jnp.zeros((8, LANES), F32)
                 ref[c, t, 120:128, :] = jnp.zeros((8, LANES), F32)
 
-    everything = wy_hot.at[pl.ds(0, 128)]
+    everything = w_edge.at[pl.ds(0, 944)]
     pltpu.make_async_copy(everything, everything, recv1).wait()
     pltpu.make_async_copy(everything, everything, send1).wait()
 
@@ -304,26 +317,45 @@
         preferred_element_type=F32,
     )
 
+    def keep_pieces(t, c, a):
+        mt[c, t, 8:120, :] = a
+        high, low = pieces(a)
+        sp[t, 112 * c : 112 * c + 112, 0:128] = high
+        sp[t, 112 * c : 112 * c + 112, 128:256] = low
+
     def assemble(t):
         for c in range(2):
             ls = slice(128 * t, 128 * t + 128)
-            mid = mv[c, :, ls]
             first, last = (r[40 * c : 40 * c + 40, ls] for r in rxf)
-            if t < 4:
-                ps = slice(512 * c + 128 * t, 512 * c + 128 * t + 128)
-                mid = mid + placed[0:96, ps]
-                first = first + placed[96:136, ps]
-                last = last + placed[144:184, ps]
-            else:
-                side = t - 4
-                mid = mid + from_y[side][c]
-                first = first + from_c[corner[0, side]][c]
-                last = last + from_c[corner[1, side]][c]
-            a = jnp.concatenate(joined(mid, first, last), axis=0)
-            mt[c, t, 8:120, :] = a
-            high, low = pieces(a)
-            sp[t, 112 * c : 112 * c + 112, 0:128] = high
-            sp[t, 112 * c : 112 * c + 112, 128:256] = low
+            ps = slice(512 * c + 128 * t, 512 * c + 128 * t + 128)
+            parts = joined(
+                mv[c, :, ls] + placed[0:96, ps],
+                first + placed[96:136, ps],
+                last + placed[144:184, ps],
+            )
+            keep_pieces(t, c, jnp.concatenate(parts, axis=0))
+
+    def outside_pieces():
+        for c in range(2):
+            first, last = (r[40 * c : 40 * c + 40, 512:640] for r in rxf)
+            whole = jnp.concatenate(joined(mv[c, :, 512:640], first, last), axis=0)
+            high, low = pieces(whole)
+            beyond[112 * c : 112 * c + 112, 0:128] = high
+            beyond[112 * c : 112 * c + 112, 128:256] = low
+
+    def assemble_strips():
+        total = jnp.dot(beyond[...], w_strip[...], preferred_element_type=F32)
+        for l in range(4):
+            total = total + jnp.dot(
+                sp[l], w_edge[256 * l : 256 * l + 256, :], preferred_element_type=F32
+            )
+        for side in range(2):
+            for c in range(2):
+                inside = joined(
+                    from_y[side][c], from_c[corner[0, side]][c], from_c[corner[1, side]][c]
+                )
+                own = total[112 * c : 112 * c + 112, 128 * side : 128 * side + 128]
+                keep_pieces(4 + side, c, own + jnp.concatenate(inside, axis=0))
 
     def advect(t):
         steps = jnp.dot(sp[t], w_adv[...], preferred_element_type=F32)
@@ -371,18 +403,18 @@
         values = [sweep(w1, beside, t, c, lo, 112 * c + lo) for lo in range(0, 112, 16)]
         return jnp.concatenate(values, axis=0)[8:104]
 
-    lane16 = lax.broadcasted_iota(jnp.int32, (16, LANES), 1)
-    j16 = lane16 % 32
-    keep = ((j16 >= 10) & (j16 < 26), (j16 >= 6) & (j16 < 22))
-    assemble(4)
-    assemble(5)
+    outside_pieces()
+    for t in range(4):
+        assemble(t)
+    advect(0)
+    assemble_strips()
+    advect(1)
     advect(4)
     advect(5)
-    assemble(0)
+    advect(2)
     first_sweep(4)
     first_sweep(5)
-    for t in (1, 2, 3):
-        assemble(t)
+    advect(3)
     for t in (4, 5):
         ls = slice(128 * (t - 4), 128 * (t - 4) + 128)
         beside = jnp.dot(sp[t], w_s[...], preferred_element_type=F32)
@@ -391,14 +423,14 @@
             high, low = pieces(whole)
             ends_in[0, 96 * c : 96 * c + 96, ls] = high
             ends_in[1, 96 * c : 96 * c + 96, ls] = low
-            kept = jnp.where(keep[t - 4], whole.reshape(6, 16, LANES), 0.0).reshape(96, LANES)
-            ta[96 * c : 96 * c + 96, 128 * t : 128 * t + 128] = kept.astype(BF)
-    for t in range(4):
-        advect(t)
+    cut = jnp.dot(ends_in[0], w_cut[...], preferred_element_type=F32)
+    ta[:, 512:640] = cut.astype(BF)
+    first_sweep(0)
+    first_sweep(1)
     ends = jnp.dot(ends_in[0], w_fix[...], preferred_element_type=F32)
     ends = ends + jnp.dot(ends_in[1], w_fix[...], preferred_element_type=F32)
-    for t in range(4):
-        first_sweep(t)
+    first_sweep(2)
+    first_sweep(3)
     lane = lax.broadcasted_iota(jnp.int32, (96, LANES), 1)
     inside = (lane >= 3) & (lane < 125)
     for t in range(4):
@@ -433,8 +465,8 @@
         functools.partial(kernel, nx, ny),
         out_shape=(
             jax.ShapeDtypeStruct((4, 2, 64, 128), F32),
-            jax.ShapeDtypeStruct((192, 768), BF),
-            jax.ShapeDtypeStruct((768, 2048), BF),
+            jax.ShapeDtypeStruct((192, 640), BF),
+            jax.ShapeDtypeStruct((640, 2048), BF),
             jax.ShapeDtypeStruct((96, 2048), F32),
         ),
         in_specs=[pl.BlockSpec(memory_space=pltpu.HBM)] * 5,
@@ -447,12 +479,12 @@
             pltpu.VMEM((6, 128), jnp.int32),
             pltpu.VMEM((23, 16, 128), F32),
             pltpu.VMEM((192, 2048), BF),
-            pltpu.VMEM((2, 96, 768), F32),
-            pltpu.VMEM((192, 768), BF),
-            pltpu.VMEM((2, 80, 768), BF),
+            pltpu.VMEM((2, 96, 640), F32),
+            pltpu.VMEM((192, 640), BF),
+            pltpu.VMEM((2, 80, 640), BF),
             pltpu.VMEM((2, 288, 128), BF),
             pltpu.VMEM((4, 128, 128), BF),
-            pltpu.VMEM((2, 80, 768), BF),
+            pltpu.VMEM((2, 80, 640), BF),
             pltpu.VMEM((2, 288, 128), BF),
             pltpu.VMEM((4, 128, 128), BF),
             pltpu.VMEM((2, 6, 128, 128), F32),
@@ -461,13 +493,17 @@
             pltpu.VMEM((6, 224, 256), BF),
             pltpu.VMEM((6, 224, 256), BF),
             pltpu.VMEM((2, 192, 256), BF),
-            pltpu.VMEM((768, 256), BF),
+            pltpu.VMEM((224, 256), BF),
             pltpu.VMEM((512, 256), BF),
+            pltpu.VMEM((256, 256), BF),
             pltpu.VMEM((256, 1024), BF),
             pltpu.VMEM((256, 256), BF),
             pltpu.VMEM((256, 128), BF),
             pltpu.VMEM((256, 128), BF),
             pltpu.VMEM((256, 512), BF),
+            pltpu.VMEM((256, 256), BF),
+            pltpu.VMEM((1024, 256), BF),
+            pltpu.VMEM((256, 128), BF),
             pltpu.SemaphoreType.DMA((5,)),
             pltpu.SemaphoreType.DMA,
             pltpu.SemaphoreType.DMA,

time: 21.3 us -> 21 us (0.986)
  Pallas kernels: 20.5 us -> 20.2 us
    pallas_call x1, Pallas kernels: 1.92 us -> 1.44 us  [body(): pl.pallas_call(sampling, out_shape=(jax.ShapeDtypeStruct((4, 2, 64, 128),...]
where the time goes in v9:
time: 21 us; the launch traced here: 20.9 us
  Pallas kernels  20.2 us (96%)
  between operations  0.64 us (3%)
    pallas_call x1, Pallas kernels, body(): pl.pallas_call(functools.partial(kernel, nx, ny), out_shape=(jax.ShapeDty...  18.8 us
    pallas_call x1, Pallas kernels, body(): pl.pallas_call(sampling, out_shape=(jax.ShapeDtypeStruct((4, 2, 64, 128),...  1.44 us

profile of v9, /device:TPU:56, one launch (start us, length us, event | category | flops | bytes accessed | tf_op | source)
XLA Modules:
  0.0 20.9 jit_solution(9751518553917580611)
XLA Ops:
  0.6 18.8 %fish_step.1 = (f32[4,2,64,128]{3,2,1,0:T(8,128)S(1)}, bf16[192,640]{1,0:T(8,128)(2,1)S(1)}, bf16[640,2048]{1,0:T(8,128)(2,1)S(1)}, f32[96,2048]{1,0:T(8,128)S(1)}) custom-call(f32[4,2,64,128]{3,2,1,0:T(8,128)} %vel_h.1, s32[3,16,128]{2,1,0:T(8,128)} %bitcast.5, f32[2,16,128]{2,1,0:T(8,128)} %bitcast.6, f32[2,16,128]{2,1,0:T(8,128)} %bitcast.7, s32[6,128]{1,0:T(8,128)} %bitcast.8), custom_call_target="tpu_custom_call" | custom-call | tf_op jit(solution)/shard_map/fish_step/pallas_call | solution.py:464
  19.4 1.4 %fish_sample.1 = (f32[4,2,64,128]{3,2,1,0:T(8,128)}, f32[2,16,128]{2,1,0:T(8,128)}) custom-call(f32[4,2,64,128]{3,2,1,0:T(8,128)S(1)} %get-tuple-element.8.v, bf16[192,640]{1,0:T(8,128)(2,1)S(1)} %get-tuple-element.9.ta, bf16[640,2048]{1,0:T(8,128)(2,1)S(1)} %get-tuple-element.10.wy_hot, f32[96,2048]{1,0:T(8,128)S(1)} %get-tuple-element.11.wx_hot), custom_call_target="tpu_custom_call" | custom-call | tf_op jit(solution)/shard_map/fish_sample/pallas_call | solution.py:523

commit v10 on v9

--- a/solution.py
+++ b/solution.py
@@ -149,7 +149,7 @@
             barrier, inc=1, device_id=at(-dx, -dy), device_id_type=pl.DeviceIdType.MESH
         )
     matrices(w_in, w_out, w_place, w_adv, w_t, w_s, w_fix, w_strip, w_edge, w_cut)
-    for load in loads:
+    for load in loads[:4]:
         load.wait()
 
     mine = jnp.where(owner[...] == ix * ny + iy, 1.0, 0.0)
@@ -171,6 +171,8 @@
             q32[10 + 4 * c + k] = force[c] * alive * wx[k]
         q32[18 + k] = jnp.where(cell[2] == k, 1.0, 0.0)
     q32[22] = alive
+
+    loads[4].wait()
 
     rows16 = lax.broadcasted_iota(jnp.int32, (16, LANES), 0).astype(F32)
     zero16 = jnp.zeros((16, LANES), BF)
@@ -406,15 +408,11 @@
     outside_pieces()
     for t in range(4):
         assemble(t)
-    advect(0)
     assemble_strips()
-    advect(1)
-    advect(4)
-    advect(5)
-    advect(2)
+    for t in range(6):
+        advect(t)
     first_sweep(4)
     first_sweep(5)
-    advect(3)
     for t in (4, 5):
         ls = slice(128 * (t - 4), 128 * (t - 4) + 128)
         beside = jnp.dot(sp[t], w_s[...], preferred_element_type=F32)
@@ -427,10 +425,10 @@
     ta[:, 512:640] = cut.astype(BF)
     first_sweep(0)
     first_sweep(1)
+    first_sweep(2)
+    first_sweep(3)
     ends = jnp.dot(ends_in[0], w_fix[...], preferred_element_type=F32)
     ends = ends + jnp.dot(ends_in[1], w_fix[...], preferred_element_type=F32)
-    first_sweep(2)
-    first_sweep(3)
     lane = lax.broadcasted_iota(jnp.int32, (96, LANES), 1)
     inside = (lane >= 3) & (lane < 125)
     for t in range(4):

time: 21 us -> 20.8 us (level)
    pallas_call x1, Pallas kernels: 18.8 us -> 18.5 us  [body(): pl.pallas_call(functools.partial(kernel, nx, ny), out_shape=(jax.ShapeDty...]
where the time goes in v10:
time: 20.8 us; the launch traced here: 20.6 us
  Pallas kernels  20 us (96%)
  between operations  0.64 us (3%)
    pallas_call x1, Pallas kernels, body(): pl.pallas_call(functools.partial(kernel, nx, ny), out_shape=(jax.ShapeDty...  18.5 us
    pallas_call x1, Pallas kernels, body(): pl.pallas_call(sampling, out_shape=(jax.ShapeDtypeStruct((4, 2, 64, 128),...  1.44 us

profile of v10, /device:TPU:56, one launch (start us, length us, event | category | flops | bytes accessed | tf_op | source)
XLA Modules:
  0.0 20.6 jit_solution(11186370504333053304)
XLA Ops:
  0.6 18.5 %fish_step.1 = (f32[4,2,64,128]{3,2,1,0:T(8,128)S(1)}, bf16[192,640]{1,0:T(8,128)(2,1)S(1)}, bf16[640,2048]{1,0:T(8,128)(2,1)S(1)}, f32[96,2048]{1,0:T(8,128)S(1)}) custom-call(f32[4,2,64,128]{3,2,1,0:T(8,128)} %vel_h.1, s32[3,16,128]{2,1,0:T(8,128)} %bitcast.5, f32[2,16,128]{2,1,0:T(8,128)} %bitcast.6, f32[2,16,128]{2,1,0:T(8,128)} %bitcast.7, s32[6,128]{1,0:T(8,128)} %bitcast.8), custom_call_target="tpu_custom_call" | custom-call | tf_op jit(solution)/shard_map/fish_step/pallas_call | solution.py:462
  19.2 1.4 %fish_sample.1 = (f32[4,2,64,128]{3,2,1,0:T(8,128)}, f32[2,16,128]{2,1,0:T(8,128)}) custom-call(f32[4,2,64,128]{3,2,1,0:T(8,128)S(1)} %get-tuple-element.8.v, bf16[192,640]{1,0:T(8,128)(2,1)S(1)} %get-tuple-element.9.ta, bf16[640,2048]{1,0:T(8,128)(2,1)S(1)} %get-tuple-element.10.wy_hot, f32[96,2048]{1,0:T(8,128)S(1)} %get-tuple-element.11.wx_hot), custom_call_target="tpu_custom_call" | custom-call | tf_op jit(solution)/shard_map/fish_sample/pallas_call | solution.py:521

commit v11 on v10

--- a/solution.py
+++ b/solution.py
@@ -238,11 +238,6 @@
         px[n] = jnp.concatenate([mv[0, lo : lo + 40, :], mv[1, lo : lo + 40, :]], axis=0).astype(BF)
 
     pl.semaphore_wait(barrier, 4)
-    for n, (dx, dy) in enumerate(UPPER):
-        pl.semaphore_signal(
-            here_sem.at[n], inc=1, device_id=at(dx, dy), device_id_type=pl.DeviceIdType.MESH
-        )
-
     def send(src, dst, dx, dy):
         copy = pltpu.make_async_remote_copy(
             src_ref=src, dst_ref=dst, send_sem=send1, recv_sem=recv1,
@@ -259,8 +254,16 @@
         else:
             send(pc.at[n - 4], rc.at[n - 4], dx, dy)
 
-    for dx, dy in UPPER[2:] + UPPER[:2][::-1]:
+    for dx, dy in UPPER[2:]:
         send_to(dx, dy)
+    for n, (dx, dy) in enumerate(UPPER):
+        pl.semaphore_signal(
+            here_sem.at[n], inc=1, device_id=at(dx, dy), device_id_type=pl.DeviceIdType.MESH
+        )
+
+    for dx, dy in UPPER[:2]:
+        send_to(dx, dy)
+
 
     for n, (dx, dy) in enumerate(UPPER):
         pl.semaphore_wait(here_sem.at[n], 1)

time: 20.8 us -> 20.7 us (level)
  no operation moved by 1% of the time
where the time goes in v11:
time: 20.7 us; the launch traced here: 20.6 us
  Pallas kernels  20 us (97%)
  between operations  0.64 us (3%)
    pallas_call x1, Pallas kernels, body(): pl.pallas_call(functools.partial(kernel, nx, ny), out_shape=(jax.ShapeDty...  18.5 us
    pallas_call x1, Pallas kernels, body(): pl.pallas_call(sampling, out_shape=(jax.ShapeDtypeStruct((4, 2, 64, 128),...  1.44 us

profile of v11, /device:TPU:56, one launch (start us, length us, event | category | flops | bytes accessed | tf_op | source)
XLA Modules:
  0.0 20.6 jit_solution(17573756450094818540)
XLA Ops:
  0.6 18.5 %fish_step.1 = (f32[4,2,64,128]{3,2,1,0:T(8,128)S(1)}, bf16[192,640]{1,0:T(8,128)(2,1)S(1)}, bf16[640,2048]{1,0:T(8,128)(2,1)S(1)}, f32[96,2048]{1,0:T(8,128)S(1)}) custom-call(f32[4,2,64,128]{3,2,1,0:T(8,128)} %vel_h.1, s32[3,16,128]{2,1,0:T(8,128)} %bitcast.5, f32[2,16,128]{2,1,0:T(8,128)} %bitcast.6, f32[2,16,128]{2,1,0:T(8,128)} %bitcast.7, s32[6,128]{1,0:T(8,128)} %bitcast.8), custom_call_target="tpu_custom_call" | custom-call | tf_op jit(solution)/shard_map/fish_step/pallas_call | solution.py:465
  19.2 1.4 %fish_sample.1 = (f32[4,2,64,128]{3,2,1,0:T(8,128)}, f32[2,16,128]{2,1,0:T(8,128)}) custom-call(f32[4,2,64,128]{3,2,1,0:T(8,128)S(1)} %get-tuple-element.8.v, bf16[192,640]{1,0:T(8,128)(2,1)S(1)} %get-tuple-element.9.ta, bf16[640,2048]{1,0:T(8,128)(2,1)S(1)} %get-tuple-element.10.wy_hot, f32[96,2048]{1,0:T(8,128)S(1)} %get-tuple-element.11.wx_hot), custom_call_target="tpu_custom_call" | custom-call | tf_op jit(solution)/shard_map/fish_sample/pallas_call | solution.py:524
